TPU v7x, 256 devices: a whole 4x4x8 slice. The times are simulated.
256 devices in a mesh: dp: 4 (over z_hi, core), expert: 64 (over x, y, z_lo).
Axes of the slice: x: 4, y: 4, z: 8 (z_hi: 2, z_lo: 4; z = z_hi * 4 + z_lo), core: 2. Of those that a mesh axis runs over, the one named last changes fastest.
Arguments:
- frames: bfloat16 [32768, 1024], P(('dp', 'expert')), may hold values from -6 to 6
- lengths: int32 [4], P('dp'), may hold values from 4096 to 8192
- expert_ids: int32 [32768, 2], P(('dp', 'expert')), may hold values from 0 to 63, all different within a row; in each aligned block of 128 rows (0 to 127, 128 to 255, ...) at most 8 rows name the same one
- capacity: int32 [64], replicated, may hold values from 4 to 8
- resident: int32 [64], replicated, may hold values from 0 to 63, each once
- partner: int32 [64], replicated, may hold values from 0 to 63, as said below
- conv_gain: float32 [1024], replicated, may hold values from 0.5 to 1.5
- conv_kernel: float32 [31, 1024], replicated, may hold values from -1 to 1
- conv_bias: float32 [1024], replicated, may hold values from -3 to 3
- ffn_gain: float32 [1024], replicated, may hold values from 0.5 to 1.5
- router: bfloat16 [1024, 64], replicated, may hold values from -0.1875 to 0.1875
- gate_weight: bfloat16 [64, 1024, 2048], P('expert', None, 'dp'), may hold values from -4 to 4
- up_weight: bfloat16 [64, 1024, 2048], P('expert', None, 'dp'), may hold values from -4 to 4
- down_weight: bfloat16 [64, 1024, 2048], P('expert', None, 'dp'), may hold values from -4 to 4
- gate_mean_grad: bfloat16 [64, 1024, 2048], P('expert', None, 'dp'), may hold values from -4 to 4
- gate_mean_square: bfloat16 [64, 1024, 2048], P('expert', None, 'dp'), may hold values from 0.25 to 4
- up_mean_grad: bfloat16 [64, 1024, 2048], P('expert', None, 'dp'), may hold values from -4 to 4
- up_mean_square: bfloat16 [64, 1024, 2048], P('expert', None, 'dp'), may hold values from 0.25 to 4
- down_mean_grad: bfloat16 [64, 1024, 2048], P('expert', None, 'dp'), may hold values from -4 to 4
- down_mean_square: bfloat16 [64, 1024, 2048], P('expert', None, 'dp'), may hold values from 0.25 to 4
Outputs:
- block_out: bfloat16 [32768, 1024], P(('dp', 'expert'))
- fresh_gate: bfloat16 [64, 1024, 2048], P('expert', None, 'dp')
- fresh_up: bfloat16 [64, 1024, 2048], P('expert', None, 'dp')
- fresh_down: bfloat16 [64, 1024, 2048], P('expert', None, 'dp')
Inputs may be any that keep to these rules, and one draw needn't show every extreme that they name: `expert_ids`: in each aligned block of 128 frames (the frames of one device) no expert is named by more than 8 choices, a bound that some block reaches. A pairing of the slots: partner[partner[d]] = d and partner[d] != d. `resident`: A permutation of the experts.
All inputs are finite; a program needn't handle non-finite values.
Results may differ from a plain program's by a relative error of at most 0.007.
Values may be sent and summed in bfloat16 or wider, within the bound.
A program may use at most 128 MiB of HBM per device.

v0:
```python
import jax
import jax.numpy as jnp
from jax import lax
from jax.sharding import PartitionSpec as P

D = 1024
FF = 2048
K = 31


LEARNING_RATE = 0.1
ADAM_EPSILON = 1e-08
NORM_EPSILON = 1e-05


def extended(cells, sides, width):
    for axis, dim in sides:
        count = lax.axis_size(axis)
        ends = count - 1
        head = lax.slice_in_dim(cells, 0, width, axis=dim)
        tail = lax.slice_in_dim(cells, cells.shape[dim] - width, cells.shape[dim], axis=dim)
        cells = jnp.concatenate(
            [
                lax.ppermute(tail, axis, [(i, (i + 1) % count) for i in range(ends)]),
                cells,
                lax.ppermute(head, axis, [((i + 1) % count, i) for i in range(ends)]),
            ],
            axis=dim,
        )
    return cells


def layer_norm(values, gain_row):
    centred = values - jnp.mean(values, axis=-1, keepdims=True)
    variance = jnp.mean(centred * centred, axis=-1, keepdims=True)
    return centred * lax.rsqrt(variance + NORM_EPSILON) * gain_row


def refresh(weight, first_moment, second_moment):
    step_size = (
        LEARNING_RATE
        * first_moment.astype(jnp.float32)
        / (jnp.sqrt(second_moment.astype(jnp.float32)) + ADAM_EPSILON)
    )
    return (weight.astype(jnp.float32) - step_size).astype(jnp.bfloat16)


def expert_part(inputs, gate_block, up_block, down_block):
    gate_pre = jnp.dot(inputs, gate_block, preferred_element_type=jnp.float32) * D ** (-0.5)
    up_pre = jnp.dot(inputs, up_block, preferred_element_type=jnp.float32) * D ** (-0.5)
    hidden = (jax.nn.silu(gate_pre) * up_pre).astype(jnp.bfloat16)
    return lax.dot_general(
        hidden, down_block, (((1,), (1,)), ((), ())), preferred_element_type=jnp.float32
    ) * FF ** (-0.5)


def shards(
    frames,
    lengths,
    expert_ids,
    capacity,
    resident,
    partner,
    conv_gain,
    conv_kernel,
    conv_bias,
    ffn_gain,
    router,
    gate_weight,
    up_weight,
    down_weight,
    gate_mean_grad,
    gate_mean_square,
    up_mean_grad,
    up_mean_square,
    down_mean_grad,
    down_mean_square,
):
    devices = lax.axis_size("expert")
    position = lax.axis_index("expert")
    frame_count = frames.shape[0]
    margin = (K - 1) // 2
    span_total = devices * frame_count

    def flatten_rows(array):
        return array.reshape(devices, -1)

    local_gate = refresh(gate_weight, gate_mean_grad, gate_mean_square)
    local_up = refresh(up_weight, up_mean_grad, up_mean_square)
    local_down = refresh(down_weight, down_mean_grad, down_mean_square)
    sent = (
        lax.all_to_all(flatten_rows(local_gate), "expert", split_axis=0, concat_axis=0, tiled=True),
        lax.all_to_all(flatten_rows(local_up), "expert", split_axis=0, concat_axis=0, tiled=True),
        lax.all_to_all(flatten_rows(local_down), "expert", split_axis=0, concat_axis=0, tiled=True),
    )
    arranged = tuple((jnp.take(piece, partner, axis=0) for piece in sent))
    landed = (
        lax.all_to_all(arranged[0], "expert", split_axis=0, concat_axis=0, tiled=True),
        lax.all_to_all(arranged[1], "expert", split_axis=0, concat_axis=0, tiled=True),
        lax.all_to_all(arranged[2], "expert", split_axis=0, concat_axis=0, tiled=True),
    )
    fresh_gate = landed[0].reshape(gate_weight.shape)
    fresh_up = landed[1].reshape(up_weight.shape)
    fresh_down = landed[2].reshape(down_weight.shape)
    start_pos = position * frame_count
    seq_length = lengths[0]
    offsets = start_pos + jnp.arange(frame_count, dtype=jnp.int32)
    live_rows = (offsets < seq_length).astype(jnp.float32)[:, None]
    inputs_f = frames.astype(jnp.float32)
    normed = (layer_norm(inputs_f, conv_gain) * live_rows).astype(jnp.bfloat16)
    padded = extended(normed, (("expert", 0),), margin)
    wide_pos = start_pos - margin + jnp.arange(frame_count + 2 * margin, dtype=jnp.int32)
    same_utterance = ((wide_pos >= 0) & (wide_pos < span_total)).astype(jnp.float32)[:, None]
    widened = padded.astype(jnp.float32) * same_utterance
    conv_sum = jnp.zeros((frame_count, frames.shape[1]), jnp.float32)
    for tap_index in range(K):
        conv_sum = conv_sum + conv_kernel[tap_index] * widened[tap_index : tap_index + frame_count]
    mixed_rows = (inputs_f + live_rows * jax.nn.silu(conv_sum + conv_bias)).astype(jnp.bfloat16)
    ffn_in = layer_norm(mixed_rows.astype(jnp.float32), ffn_gain).astype(jnp.bfloat16)
    logits = jnp.dot(ffn_in, router, preferred_element_type=jnp.float32)
    expert_iota = jnp.arange(router.shape[1], dtype=jnp.int32)
    picked = expert_ids[:, :, None] == expert_iota[None, None, :]
    chosen = jnp.sum(jnp.where(picked, logits[:, None, :], 0.0), axis=-1)
    scores = jax.nn.sigmoid(chosen)
    gate_values = (scores / jnp.sum(scores, axis=-1, keepdims=True)).astype(jnp.bfloat16)
    holder = jnp.take(resident, partner)
    new_slot = jnp.sum(
        jnp.where(holder[None, :] == expert_iota[:, None], expert_iota[None, :], 0), axis=1
    )
    flat_ids = expert_ids.reshape(-1)
    onehot = (flat_ids[:, None] == expert_iota[None, :]).astype(jnp.int32)
    earlier = jnp.cumsum(onehot, axis=0) - onehot
    rank_in_block = jnp.sum(earlier * onehot, axis=1)
    slot_limit = jnp.sum(onehot * capacity[None, :], axis=1)
    dest_slot = jnp.sum(onehot * new_slot[None, :], axis=1)
    kept_pairs = rank_in_block < slot_limit
    cap_slots = 4 * frame_count // devices
    total_slots = devices * cap_slots
    slot_index = dest_slot * cap_slots + rank_in_block
    selected = (
        slot_index[:, None] == jnp.arange(total_slots, dtype=jnp.int32)[None, :]
    ) & kept_pairs[:, None]
    selected = selected.reshape(frame_count, expert_ids.shape[1], total_slots)
    dispatch_rows = jnp.any(selected, axis=1).astype(jnp.bfloat16)
    combine_rows = jnp.sum(
        jnp.where(selected, gate_values[:, :, None].astype(jnp.float32), 0.0), axis=1
    ).astype(jnp.bfloat16)
    outgoing = lax.dot_general(
        dispatch_rows, ffn_in, (((0,), (0,)), ((), ())), preferred_element_type=jnp.float32
    )
    outgoing = outgoing.astype(jnp.bfloat16).reshape(devices, cap_slots, frames.shape[1])
    gate_local = fresh_gate[0]
    up_local = fresh_up[0]
    down_local = fresh_down[0]
    arrived = lax.all_to_all(outgoing, "expert", split_axis=0, concat_axis=0, tiled=True)
    flat_rows = arrived.reshape(-1, arrived.shape[-1])
    everyone = lax.all_gather(flat_rows, "dp", axis=0, tiled=True)
    summed = lax.psum_scatter(
        expert_part(everyone, gate_local, up_local, down_local).astype(jnp.bfloat16),
        "dp",
        scatter_dimension=0,
        tiled=True,
    )
    results = summed.reshape(arrived.shape)
    returned = lax.all_to_all(results, "expert", split_axis=0, concat_axis=0, tiled=True)
    moe_sum = jnp.dot(
        combine_rows, returned.reshape(total_slots, -1), preferred_element_type=jnp.float32
    )
    block_out = (mixed_rows.astype(jnp.float32) + 0.5 * moe_sum).astype(jnp.bfloat16)
    return (block_out, fresh_gate, fresh_up, fresh_down)


def solution(mesh):
    placed = (
        P(("dp", "expert"), None),
        P("dp"),
        P(("dp", "expert"), None),
        P(),
        P(),
        P(),
        P(),
        P(),
        P(),
        P(),
        P(),
        P("expert", None, "dp"),
        P("expert", None, "dp"),
        P("expert", None, "dp"),
        P("expert", None, "dp"),
        P("expert", None, "dp"),
        P("expert", None, "dp"),
        P("expert", None, "dp"),
        P("expert", None, "dp"),
        P("expert", None, "dp"),
    )
    return jax.shard_map(
        shards,
        mesh=mesh,
        in_specs=placed,
        out_specs=(
            P(("dp", "expert"), None),
            P("expert", None, "dp"),
            P("expert", None, "dp"),
            P("expert", None, "dp"),
        ),
        check_vma=False,
    )
```

profile of v0, /device:TPU:2, one launch (start us, length us, event | category | flops | bytes accessed | tf_op | source)
XLA Modules:
  0.0 477.7 jit_solution(5746097353587669341)
XLA Ops:
  7.2 2.9 subtract_convert_fusion.2
  11.3 7.1 %reduce.10 = bf16[64,8192]{1,0:T(8,128)(2,1)S(1)} reduce(bf16[64,1,8192]{2,1,0:T(2,128)(2,1)S(1)} %all_to_all.65, bf16[]{:T(256)} %broadcast.192), dimensions={1}, to_apply=%all_to_all.65.reduce_sub_computation | reduce | bytes 2097154 | tf_op jit(solution)/shard_map/all_to_all | solution.py:92
  18.5 1.6 reshape.248
  20.0 12.4 %all-to-all-start.1 = ((bf16[64,2,4096]{2,1,0:T(2,128)(2,1)}), bf16[64,2,4096]{2,1,0:T(2,128)(2,1)S(1)}, u32[]{:S(2)}, u32[]{:S(2)}) async-start(bf16[64,2,4096]{2,1,0:T(2,128)(2,1)} %reshape.248), calls=%async_computation.1 | async-start | bytes 2097152 | tf_op jit(solution)/shard_map/all_to_all | solution.py:92
  33.1 3.2 subtract_convert_fusion.1
  36.4 4.0 all_to_all.66
  40.4 8.2 %reduce.8 = bf16[64,8192]{1,0:T(8,128)(2,1)} reduce(bf16[64,1,8192]{2,1,0:T(2,128)(2,1)S(1)} %all_to_all.66, bf16[]{:T(256)} %broadcast.192), dimensions={1}, to_apply=%all_to_all.66.reduce_sub_computation | reduce | bytes 2097154 | tf_op jit(solution)/shard_map/all_to_all | solution.py:93
  48.6 2.6 reshape.252
  51.8 8.7 %all-to-all-done.1 = bf16[64,2,4096]{2,1,0:T(2,128)(2,1)S(1)} async-done(((bf16[64,2,4096]{2,1,0:T(2,128)(2,1)}), bf16[64,2,4096]{2,1,0:T(2,128)(2,1)S(1)}, u32[]{:S(2)}, u32[]{:S(2)}) %all-to-all-start.1) | async-done | bytes 1048608 | tf_op jit(solution)/shard_map/all_to_all | solution.py:92
  60.5 6.8 %all-to-all-start.3 = ((bf16[64,2,4096]{2,1,0:T(2,128)(2,1)}), bf16[64,2,4096]{2,1,0:T(2,128)(2,1)}, u32[]{:S(2)}, u32[]{:S(2)}) async-start(bf16[64,2,4096]{2,1,0:T(2,128)(2,1)} %reshape.252), calls=%async_computation.3 | async-start | bytes 2097152 | tf_op jit(solution)/shard_map/all_to_all | solution.py:93
  67.9 3.4 collective-permute-start
  71.3 7.5 %collective-permute-start.1 = (bf16[15,1024]{1,0:T(8,128)(2,1)}, bf16[15,1024]{1,0:T(8,128)(2,1)}, u32[]{:S(2)}, u32[]{:S(2)}) collective-permute-start(bf16[15,1024]{1,0:T(8,128)(2,1)} %get-tuple-element.13), channel_id=1, source_target_pairs={{1,0},{2,1},{3,2},{4,3},{5,4},{6,5},{7,6},{8,7},{9,8},{10,9},{11,1... | collective-permute-start | bytes 92168 | tf_op jit(solution)/shard_map/ppermute | solution.py:26
  80.4 3.6 subtract_convert_fusion
  84.0 4.0 all_to_all.67
  88.1 7.4 %reduce.9 = bf16[64,8192]{1,0:T(8,128)(2,1)S(1)} reduce(bf16[64,1,8192]{2,1,0:T(2,128)(2,1)S(1)} %all_to_all.67, bf16[]{:T(256)} %broadcast.192), dimensions={1}, to_apply=%all_to_all.67.reduce_sub_computation | reduce | bytes 2097154 | tf_op jit(solution)/shard_map/all_to_all | solution.py:94
  95.5 1.6 reshape.244
  98.9 6.5 %all-to-all-start.5 = ((bf16[64,2,4096]{2,1,0:T(2,128)(2,1)}), bf16[64,2,4096]{2,1,0:T(2,128)(2,1)S(1)}, u32[]{:S(2)}, u32[]{:S(2)}) async-start(bf16[64,2,4096]{2,1,0:T(2,128)(2,1)} %reshape.244), calls=%async_computation.5 | async-start | bytes 2097152 | tf_op jit(solution)/shard_map/all_to_all | solution.py:94
  106.1 0.9 convert_multiply_fusion
  107.0 3.9 convert_reduce_fusion
  111.2 1.6 fusion
  112.8 18.4 %all-to-all-done.5 = bf16[64,2,4096]{2,1,0:T(2,128)(2,1)S(1)} async-done(((bf16[64,2,4096]{2,1,0:T(2,128)(2,1)}), bf16[64,2,4096]{2,1,0:T(2,128)(2,1)S(1)}, u32[]{:S(2)}, u32[]{:S(2)}) %all-to-all-start.5) | async-done | bytes 1048608 | tf_op jit(solution)/shard_map/all_to_all | solution.py:94
  131.2 6.8 %all-to-all-start = ((bf16[64,8,1024]{2,1,0:T(8,128)(2,1)}), bf16[64,8,1024]{2,1,0:T(8,128)(2,1)}, u32[]{:S(2)}, u32[]{:S(2)}) async-start(bf16[64,8,1024]{2,1,0:T(8,128)(2,1)} %fusion), calls=%async_computation | async-start | bytes 2097152 | tf_op jit(solution)/shard_map/all_to_all | solution.py:155
  138.0 1.1 reshape.249
  139.1 1.1 copy.71
  140.3 2.2 gather_fusion.1
  142.4 6.5 %reshape.253 = bf16[64,1,8192]{2,1,0:T(2,128)(2,1)S(1)} reshape(bf16[64,2,4096]{2,1,0:T(2,128)(2,1)} %all-to-all-done.3) | data formatting | bytes 2097152
  148.9 1.1 copy.70
  150.1 2.2 gather_fusion.2
  152.3 6.5 %reshape.245 = bf16[64,1,8192]{2,1,0:T(2,128)(2,1)S(1)} reshape(bf16[64,2,4096]{2,1,0:T(2,128)(2,1)} %copy-done.8) | data formatting | bytes 2097152
  158.8 1.1 copy.69
  159.9 2.2 gather_fusion.3
  162.1 2.1 all-to-all-done
  164.2 2.9 select_bitcast_fusion.1
  167.1 2.7 reduce.12
  169.8 1.6 reshape.250
  171.4 8.8 %all-to-all-start.2 = ((bf16[64,2,4096]{2,1,0:T(2,128)(2,1)}), bf16[64,2,4096]{2,1,0:T(2,128)(2,1)S(1)}, u32[]{:S(2)}, u32[]{:S(2)}) async-start(bf16[64,2,4096]{2,1,0:T(2,128)(2,1)} %reshape.250), calls=%async_computation.2 | async-start | bytes 2097152 | tf_op jit(solution)/shard_map/all_to_all | solution.py:98
  180.1 2.1 reduce.13
  182.2 2.6 reshape.254
  184.8 65.4 %all-to-all-done.2 = bf16[64,2,4096]{2,1,0:T(2,128)(2,1)S(1)} async-done(((bf16[64,2,4096]{2,1,0:T(2,128)(2,1)}), bf16[64,2,4096]{2,1,0:T(2,128)(2,1)S(1)}, u32[]{:S(2)}, u32[]{:S(2)}) %all-to-all-start.2) | async-done | bytes 1048608 | tf_op jit(solution)/shard_map/all_to_all | solution.py:98
  250.2 6.3 %all-to-all-start.4 = ((bf16[64,2,4096]{2,1,0:T(2,128)(2,1)}), bf16[64,2,4096]{2,1,0:T(2,128)(2,1)S(1)}, u32[]{:S(2)}, u32[]{:S(2)}) async-start(bf16[64,2,4096]{2,1,0:T(2,128)(2,1)} %reshape.254), calls=%async_computation.4 | async-start | bytes 2097152 | tf_op jit(solution)/shard_map/all_to_all | solution.py:99
  256.6 2.1 reduce.11
  258.6 2.6 reshape.246
  261.3 23.4 %all-to-all-done.4 = bf16[64,2,4096]{2,1,0:T(2,128)(2,1)S(1)} async-done(((bf16[64,2,4096]{2,1,0:T(2,128)(2,1)}), bf16[64,2,4096]{2,1,0:T(2,128)(2,1)S(1)}, u32[]{:S(2)}, u32[]{:S(2)}) %all-to-all-start.4) | async-done | bytes 1048608 | tf_op jit(solution)/shard_map/all_to_all | solution.py:99
  284.7 6.8 %all-to-all-start.6 = ((bf16[64,2,4096]{2,1,0:T(2,128)(2,1)}), bf16[64,2,4096]{2,1,0:T(2,128)(2,1)}, u32[]{:S(2)}, u32[]{:S(2)}) async-start(bf16[64,2,4096]{2,1,0:T(2,128)(2,1)} %reshape.246), calls=%async_computation.6 | async-start | bytes 2097152 | tf_op jit(solution)/shard_map/all_to_all | solution.py:100
  291.5 1.1 reshape.251
  292.6 6.5 %reduce.1 = bf16[64,8192]{1,0:T(8,128)(2,1)S(1)} reduce(bf16[64,1,8192]{2,1,0:T(2,128)(2,1)S(1)} %reshape.251, bf16[]{:T(256)} %constant.88), dimensions={1}, to_apply=%all_to_all.53.reduce_sub_computation | reduce | bytes 2097154 | tf_op jit(solution)/shard_map/all_to_all | solution.py:98
  299.1 1.3 squeeze_reshape.9
  300.5 3.7 reshape.255
  304.1 7.9 %reduce.2 = bf16[64,8192]{1,0:T(8,128)(2,1)S(1)} reduce(bf16[64,1,8192]{2,1,0:T(2,128)(2,1)} %reshape.255, bf16[]{:T(256)} %constant.88), dimensions={1}, to_apply=%all_to_all.58.reduce_sub_computation | reduce | bytes 2097154 | tf_op jit(solution)/shard_map/all_to_all | solution.py:99
  312.0 1.4 squeeze_reshape.10
  313.4 5.1 %all-to-all-done.6 = bf16[64,2,4096]{2,1,0:T(2,128)(2,1)} async-done(((bf16[64,2,4096]{2,1,0:T(2,128)(2,1)}), bf16[64,2,4096]{2,1,0:T(2,128)(2,1)}, u32[]{:S(2)}, u32[]{:S(2)}) %all-to-all-start.6) | async-done | bytes 1048608 | tf_op jit(solution)/shard_map/all_to_all | solution.py:100
  318.4 7.5 %reshape.247 = bf16[64,1,8192]{2,1,0:T(2,128)(2,1)} reshape(bf16[64,2,4096]{2,1,0:T(2,128)(2,1)} %all-to-all-done.6) | data formatting | bytes 2097152
  325.9 7.9 %reduce.3 = bf16[64,8192]{1,0:T(8,128)(2,1)S(1)} reduce(bf16[64,1,8192]{2,1,0:T(2,128)(2,1)} %reshape.247, bf16[]{:T(256)} %constant.88), dimensions={1}, to_apply=%all_to_all.63.reduce_sub_computation | reduce | bytes 2097154 | tf_op jit(solution)/shard_map/all_to_all | solution.py:100
  333.8 1.5 squeeze_reshape.11
  335.4 6.8 %fusion.65 = f32[2048,512]{1,0:T(8,128)} fusion(bf16[2048,1024]{1,0:T(8,128)(2,1)} %all-gather.2.cloned.1.call-done, bf16[1024,512]{1,0:T(8,128)(2,1)} %squeeze_reshape.9), kind=kOutput, calls=%fused_computation.143 | convolution fusion | flops 2147483648 | bytes 9437184 | tf_op jit(solution)/shard_map/dot_general | solution.py:49
  342.2 11.2 %multiply_convert_fusion = bf16[2048,1024]{1,0:T(8,128)(2,1)} fusion(bf16[1024,512]{1,0:T(8,128)(2,1)} %squeeze_reshape.11, f32[2048,512]{1,0:T(8,128)} %fusion.65, bf16[2048,1024]{1,0:T(8,128)(2,1)} %all-gather.2.cloned.1.call-done, bf16[1024,512]{1,0:T(8,128)(2,1)} %squeeze_reshape.10), kind=kOutput, calls=%fused_computation.4 | convolution fusion | flops 4307550208 | bytes 14680064 | tf_op jit(solution)/shard_map/dot_general | solution.py:52
  353.4 78.7 %reduce-scatter.2.cloned.1.call-done = bf16[512,1024]{1,0:T(8,128)(2,1)} async-done(((bf16[2048,1024]{1,0:T(8,128)(2,1)}), bf16[512,1024]{1,0:T(8,128)(2,1)}) %reduce-scatter.2.cloned.1.call-update) | async-done | bytes 1048592 | tf_op jit(solution)/shard_map/reduce_scatter | solution.py:158
  432.1 8.0 %all-to-all-start.7 = ((bf16[64,8,1024]{2,1,0:T(8,128)(2,1)}), bf16[64,8,1024]{2,1,0:T(8,128)(2,1)}, u32[]{:S(2)}, u32[]{:S(2)}) async-start(bf16[64,8,1024]{2,1,0:T(8,128)(2,1)} %bitcast.85), calls=%async_computation.8 | async-start | bytes 2097152 | tf_op jit(solution)/shard_map/all_to_all | solution.py:165
  440.2 0.9 fusion.59
  442.0 1.3 reshape.192
  443.3 1.3 reshape.193
  444.6 1.3 reshape.194
  445.9 22.3 %all-to-all-done.7 = bf16[64,8,1024]{2,1,0:T(8,128)(2,1)} async-done(((bf16[64,8,1024]{2,1,0:T(8,128)(2,1)}), bf16[64,8,1024]{2,1,0:T(8,128)(2,1)}, u32[]{:S(2)}, u32[]{:S(2)}) %all-to-all-start.7) | async-done | bytes 1048608 | tf_op jit(solution)/shard_map/all_to_all | solution.py:165
  468.2 2.2 fusion.2
  (119 shorter events, 7.8 us)
Async XLA Ops:
  7.2 433.0 %copy-start = (bf16[1024,64]{0,1:T(8,128)(2,1)S(1)}, bf16[1024,64]{0,1:T(8,128)(2,1)}, u32[]{:S(2)}) copy-start(bf16[1024,64]{0,1:T(8,128)(2,1)} %param.32) | copy-start | bytes 393220
  18.4 14.6 %copy-start.15 = (bf16[1,1024,512]{2,1,0:T(8,128)(2,1)S(1)}, bf16[1,1024,512]{2,1,0:T(8,128)(2,1)}, u32[]{:S(2)}) copy-start(bf16[1,1024,512]{2,1,0:T(8,128)(2,1)} %param.39) | copy-start | bytes 3145732
  18.5 14.6 %copy-start.16 = (bf16[1,1024,512]{2,1,0:T(8,128)(2,1)S(1)}, bf16[1,1024,512]{2,1,0:T(8,128)(2,1)}, u32[]{:S(2)}) copy-start(bf16[1,1024,512]{2,1,0:T(8,128)(2,1)} %param.38) | copy-start | bytes 3145732
  20.0 40.4 %all-to-all-start.1 = ((bf16[64,2,4096]{2,1,0:T(2,128)(2,1)}), bf16[64,2,4096]{2,1,0:T(2,128)(2,1)S(1)}, u32[]{:S(2)}, u32[]{:S(2)}) async-start(bf16[64,2,4096]{2,1,0:T(2,128)(2,1)} %reshape.248), calls=%async_computation.1 | async-start | bytes 2097152 | tf_op jit(solution)/shard_map/all_to_all | solution.py:92
  40.4 10.8 %copy-start.2 = (bf16[128,1024]{1,0:T(8,128)(2,1)S(1)}, bf16[128,1024]{1,0:T(8,128)(2,1)}, u32[]{:S(2)}) copy-start(bf16[128,1024]{1,0:T(8,128)(2,1)} %param.22) | copy-start | bytes 786436
  48.6 3.0 copy-start.23
  51.2 27.6 %copy-start.26 = (s32[128,2]{0,1:T(2,128)S(1)}, s32[128,2]{0,1:T(2,128)}, u32[]{:S(2)}) copy-start(s32[128,2]{0,1:T(2,128)} %param.24) | copy-start | bytes 3076
  51.2 29.2 %copy-start.17 = (bf16[1,1024,512]{2,1,0:T(8,128)(2,1)S(1)}, bf16[1,1024,512]{2,1,0:T(8,128)(2,1)}, u32[]{:S(2)}) copy-start(bf16[1,1024,512]{2,1,0:T(8,128)(2,1)} %param.41) | copy-start | bytes 3145732
  51.2 20.1 %copy-start.28 = (f32[128]{0:T(128)}, f32[128]{0:T(128)S(1)}, u32[]{:S(2)}) copy-start(f32[128]{0:T(128)S(1)} %compare_convert_fusion) | copy-start | bytes 1540
  51.8 28.2 %copy-start.13 = (bf16[128,1024]{1,0:T(8,128)(2,1)}, bf16[128,1024]{1,0:T(8,128)(2,1)S(1)}, u32[]{:S(2)}) copy-start(bf16[128,1024]{1,0:T(8,128)(2,1)S(1)} %fusion.14) | copy-start | bytes 786436
  60.5 23.5 %copy-start.6 = (bf16[64,2,4096]{2,1,0:T(2,128)(2,1)}, bf16[64,2,4096]{2,1,0:T(2,128)(2,1)S(1)}, u32[]{:S(2)}) copy-start(bf16[64,2,4096]{2,1,0:T(2,128)(2,1)S(1)} %all-to-all-done.1) | copy-start | bytes 3145732
  60.5 38.4 %all-to-all-start.3 = ((bf16[64,2,4096]{2,1,0:T(2,128)(2,1)}), bf16[64,2,4096]{2,1,0:T(2,128)(2,1)}, u32[]{:S(2)}, u32[]{:S(2)}) async-start(bf16[64,2,4096]{2,1,0:T(2,128)(2,1)} %reshape.252), calls=%async_computation.3 | async-start | bytes 2097152 | tf_op jit(solution)/shard_map/all_to_all | solution.py:93
  67.9 38.2 %collective-permute-start = (bf16[15,1024]{1,0:T(8,128)(2,1)}, bf16[15,1024]{1,0:T(8,128)(2,1)}, u32[]{:S(2)}, u32[]{:S(2)}) collective-permute-start(bf16[15,1024]{1,0:T(8,128)(2,1)} %get-tuple-element.12), channel_id=1, source_target_pairs={{0,1},{1,2},{2,3},{3,4},{4,5},{5,6},{6,7},{7,8},{8,9},{9,10},{10,1... | collective-permute-start | bytes 92168 | tf_op jit(solution)/shard_map/ppermute | solution.py:24
  71.3 34.8 %collective-permute-start.1 = (bf16[15,1024]{1,0:T(8,128)(2,1)}, bf16[15,1024]{1,0:T(8,128)(2,1)}, u32[]{:S(2)}, u32[]{:S(2)}) collective-permute-start(bf16[15,1024]{1,0:T(8,128)(2,1)} %get-tuple-element.13), channel_id=1, source_target_pairs={{1,0},{2,1},{3,2},{4,3},{5,4},{6,5},{7,6},{8,7},{9,8},{10,9},{11,1... | collective-permute-start | bytes 92168 | tf_op jit(solution)/shard_map/ppermute | solution.py:26
  79.8 0.6 copy-start.18
  80.0 4.0 copy-start.22
  88.0 9.1 %copy-start.33 = (s32[64]{0:T(128)S(1)}, s32[64]{0:T(128)}, u32[]{:S(2)}) copy-start(s32[64]{0:T(128)} %param.27) | copy-start | bytes 772
  88.0 9.1 %copy-start.1 = (s32[64]{0:T(128)S(1)}, s32[64]{0:T(128)}, u32[]{:S(2)}) copy-start(s32[64]{0:T(128)} %param.26) | copy-start | bytes 772
  95.4 2.5 copy-start.34
  95.5 3.2 copy-start.19
  95.5 3.2 slice-start
  95.5 3.2 copy-start.31
  95.5 3.3 copy-start.21
  97.1 9.0 %copy-start.14 = (bf16[128,1024]{1,0:T(8,128)(2,1)S(1)}, bf16[128,1024]{1,0:T(8,128)(2,1)}, u32[]{:S(2)}) copy-start(bf16[128,1024]{1,0:T(8,128)(2,1)} %copy-done.13) | copy-start | bytes 786436
  97.1 9.9 %copy-start.24 = (f32[1024]{0:T(1024)S(1)}, f32[1024]{0:T(1024)}, u32[]{:S(2)}) copy-start(f32[1024]{0:T(1024)} %param.30) | copy-start | bytes 12292
  97.1 9.9 %copy-start.29 = (f32[128]{0:T(128)S(1)}, f32[128]{0:T(128)}, u32[]{:S(2)}) copy-start(f32[128]{0:T(128)} %copy-done.28) | copy-start | bytes 1540
  98.9 32.3 %all-to-all-start.5 = ((bf16[64,2,4096]{2,1,0:T(2,128)(2,1)}), bf16[64,2,4096]{2,1,0:T(2,128)(2,1)S(1)}, u32[]{:S(2)}, u32[]{:S(2)}) async-start(bf16[64,2,4096]{2,1,0:T(2,128)(2,1)} %reshape.244), calls=%async_computation.5 | async-start | bytes 2097152 | tf_op jit(solution)/shard_map/all_to_all | solution.py:94
  107.0 4.2 copy-start.25
  110.9 27.1 %copy-start.7 = (bf16[64,2,4096]{2,1,0:T(2,128)(2,1)S(1)}, bf16[64,2,4096]{2,1,0:T(2,128)(2,1)}, u32[]{:S(2)}) copy-start(bf16[64,2,4096]{2,1,0:T(2,128)(2,1)} %copy-done.6) | copy-start | bytes 3145732
  111.0 27.0 %copy-start.30 = (f32[128]{0:T(128)}, f32[128]{0:T(128)S(1)}, u32[]{:S(2)}) copy-start(f32[128]{0:T(128)S(1)} %broadcast_multiply_fusion) | copy-start | bytes 1540
  111.2 26.8 %copy-start.32 = (f32[128]{0:T(128)}, f32[128]{0:T(128)S(1)}, u32[]{:S(2)}) copy-start(f32[128]{0:T(128)S(1)} %add_rsqrt_fusion) | copy-start | bytes 1540
  131.2 6.8 %copy-start.8 = (bf16[64,2,4096]{2,1,0:T(2,128)(2,1)}, bf16[64,2,4096]{2,1,0:T(2,128)(2,1)S(1)}, u32[]{:S(2)}) copy-start(bf16[64,2,4096]{2,1,0:T(2,128)(2,1)S(1)} %all-to-all-done.5) | copy-start | bytes 3145732
  131.2 33.0 %all-to-all-start = ((bf16[64,8,1024]{2,1,0:T(8,128)(2,1)}), bf16[64,8,1024]{2,1,0:T(8,128)(2,1)}, u32[]{:S(2)}, u32[]{:S(2)}) async-start(bf16[64,8,1024]{2,1,0:T(8,128)(2,1)} %fusion), calls=%async_computation | async-start | bytes 2097152 | tf_op jit(solution)/shard_map/all_to_all | solution.py:155
  138.0 197.4 %all-gather.2.cloned.1.call-start = ((), (), s32[]{:S(2)}) async-start(), calls=%async_computation.9 | async-start | bytes 5242880 | tf_op jit(solution)/shard_map/all_gather | solution.py:157
  159.9 4.3 copy-start.3
  159.9 4.3 copy-start.4
  169.8 10.4 %copy-start.5 = (bf16[64,1,8192]{2,0,1:T(8,128)(2,1)S(1)}, bf16[64,1,8192]{2,0,1:T(8,128)(2,1)}, u32[]{:S(2)}) copy-start(bf16[64,1,8192]{2,0,1:T(8,128)(2,1)} %get-tuple-element.45) | copy-start | bytes 3145732
  171.4 78.9 %all-to-all-start.2 = ((bf16[64,2,4096]{2,1,0:T(2,128)(2,1)}), bf16[64,2,4096]{2,1,0:T(2,128)(2,1)S(1)}, u32[]{:S(2)}, u32[]{:S(2)}) async-start(bf16[64,2,4096]{2,1,0:T(2,128)(2,1)} %reshape.250), calls=%async_computation.2 | async-start | bytes 2097152 | tf_op jit(solution)/shard_map/all_to_all | solution.py:98
  250.2 8.4 %copy-start.9 = (bf16[64,2,4096]{2,1,0:T(2,128)(2,1)}, bf16[64,2,4096]{2,1,0:T(2,128)(2,1)S(1)}, u32[]{:S(2)}) copy-start(bf16[64,2,4096]{2,1,0:T(2,128)(2,1)S(1)} %all-to-all-done.2) | copy-start | bytes 3145732
  250.2 34.5 %all-to-all-start.4 = ((bf16[64,2,4096]{2,1,0:T(2,128)(2,1)}), bf16[64,2,4096]{2,1,0:T(2,128)(2,1)S(1)}, u32[]{:S(2)}, u32[]{:S(2)}) async-start(bf16[64,2,4096]{2,1,0:T(2,128)(2,1)} %reshape.254), calls=%async_computation.4 | async-start | bytes 2097152 | tf_op jit(solution)/shard_map/all_to_all | solution.py:99
  261.3 30.3 %copy-start.10 = (bf16[64,2,4096]{2,1,0:T(2,128)(2,1)S(1)}, bf16[64,2,4096]{2,1,0:T(2,128)(2,1)}, u32[]{:S(2)}) copy-start(bf16[64,2,4096]{2,1,0:T(2,128)(2,1)} %copy-done.9) | copy-start | bytes 3145732
  284.7 6.8 %copy-start.11 = (bf16[64,2,4096]{2,1,0:T(2,128)(2,1)}, bf16[64,2,4096]{2,1,0:T(2,128)(2,1)S(1)}, u32[]{:S(2)}) copy-start(bf16[64,2,4096]{2,1,0:T(2,128)(2,1)S(1)} %all-to-all-done.4) | copy-start | bytes 3145732
  284.7 33.7 %all-to-all-start.6 = ((bf16[64,2,4096]{2,1,0:T(2,128)(2,1)}), bf16[64,2,4096]{2,1,0:T(2,128)(2,1)}, u32[]{:S(2)}, u32[]{:S(2)}) async-start(bf16[64,2,4096]{2,1,0:T(2,128)(2,1)} %reshape.246), calls=%async_computation.6 | async-start | bytes 2097152 | tf_op jit(solution)/shard_map/all_to_all | solution.py:100
  291.5 140.6 %reduce-scatter.2.cloned.1.call-start = ((), (), s32[]{:S(2)}) async-start(), calls=%async_computation.10 | async-start | bytes 5242880 | tf_op jit(solution)/shard_map/reduce_scatter | solution.py:158
  299.1 1.3 copy-start.12
  353.4 87.7 %copy-start.27 = (s32[128,2]{0,1:T(2,128)S(1)}, s32[128,2]{0,1:T(2,128)}, u32[]{:S(2)}) copy-start(s32[128,2]{0,1:T(2,128)} %param.24) | copy-start | bytes 3076
  432.1 36.1 %all-to-all-start.7 = ((bf16[64,8,1024]{2,1,0:T(8,128)(2,1)}), bf16[64,8,1024]{2,1,0:T(8,128)(2,1)}, u32[]{:S(2)}, u32[]{:S(2)}) async-start(bf16[64,8,1024]{2,1,0:T(8,128)(2,1)} %bitcast.85), calls=%async_computation.8 | async-start | bytes 2097152 | tf_op jit(solution)/shard_map/all_to_all | solution.py:165
  443.3 24.9 %copy-start.20 = (bf16[128,512]{1,0:T(8,128)(2,1)S(1)}, bf16[128,512]{1,0:T(8,128)(2,1)}, u32[]{:S(2)}) copy-start(bf16[128,512]{1,0:T(8,128)(2,1)} %select_reduce_fusion) | copy-start | bytes 393220
Sparse Core Ops, SparseCore 0:
  164.3 81.1 all-gather.1
  353.5 78.5 reduce-scatter.1
where the time goes:
time: 487 us; the launch traced here: 478 us
  waiting for transfers between devices  224 us (46%)
  starting transfers between devices  73.2 us (15%)
  other arithmetic  72.5 us (15%)
  local copies, waits for them, and re-layouts  69.2 us (14%)
  matrix products  22.7 us (5%)
  between operations  15.9 us (3%)
    reduce_scatter x1, waiting for transfers between devices, shards(): lax.psum_scatter(expert_part(everyone, gate_local, up_local, down_local)....  78.7 us
    all_to_all x1, waiting for transfers between devices, shards(): lax.all_to_all(arranged[0], 'expert', split_axis=0, concat_axis=0, tiled=...  65.4 us
    unnamed x86, local copies, waits for them, and re-layouts  43 us
    all_to_all x1, waiting for transfers between devices, shards(): lax.all_to_all(arranged[1], 'expert', split_axis=0, concat_axis=0, tiled=...  23.4 us
    all_to_all x1, waiting for transfers between devices, shards(): lax.all_to_all(results, 'expert', split_axis=0, concat_axis=0, tiled=True)  22.3 us
    all_to_all x1, waiting for transfers between devices, shards(): lax.all_to_all(flatten_rows(local_down), 'expert', split_axis=0, concat_a...  18.4 us
    all_to_all x3, other arithmetic, shards(): lax.all_to_all(arranged[1], 'expert', split_axis=0, concat_axis=0, tiled=...  12.8 us
    all_to_all x1, starting transfers between devices, shards(): lax.all_to_all(flatten_rows(local_gate), 'expert', split_axis=0, concat_a...  12.4 us
  transfers between devices with their start and end apart: 12, of which 8 were waited for; matrix products, arithmetic and copies ran while one was open for 26% of the time, Pallas kernels for 0%

commit v1 on v0

v1 whole, which is shorter than its diff:
```python
import functools

import jax
import jax.numpy as jnp
from jax import lax
from jax.experimental import pallas as pl
from jax.experimental.pallas import tpu as pltpu
from jax.sharding import PartitionSpec as P

D = 1024
FF = 2048
K = 31


LEARNING_RATE = 0.1
ADAM_EPSILON = 1e-08
NORM_EPSILON = 1e-05

MESH = pl.DeviceIdType.MESH
XY = 16
ZL = 4
ZN = 8
HALF = ZN // 2
GROUP = XY * ZL
SLOTS = 8
TOK = 128
FLOC = 512
ROWS = XY * 2 * SLOTS
PIECE = D // GROUP


def extended(cells, sides, width):
    for axis, dim in sides:
        count = lax.axis_size(axis)
        ends = count - 1
        head = lax.slice_in_dim(cells, 0, width, axis=dim)
        tail = lax.slice_in_dim(cells, cells.shape[dim] - width, cells.shape[dim], axis=dim)
        cells = jnp.concatenate(
            [
                lax.ppermute(tail, axis, [(i, (i + 1) % count) for i in range(ends)]),
                cells,
                lax.ppermute(head, axis, [((i + 1) % count, i) for i in range(ends)]),
            ],
            axis=dim,
        )
    return cells


def layer_norm(values, gain_row):
    centred = values - jnp.mean(values, axis=-1, keepdims=True)
    variance = jnp.mean(centred * centred, axis=-1, keepdims=True)
    return centred * lax.rsqrt(variance + NORM_EPSILON) * gain_row


def refresh(weight, first_moment, second_moment):
    step_size = (
        LEARNING_RATE
        * first_moment.astype(jnp.float32)
        / (jnp.sqrt(second_moment.astype(jnp.float32)) + ADAM_EPSILON)
    )
    return (weight.astype(jnp.float32) - step_size).astype(jnp.bfloat16)


def silu(value):
    return value / (1.0 + jnp.exp(-value))


def kernel(
    partner_ref,
    ffn_ref,
    mixed_ref,
    meta_ref,
    gw, gm, gs, uw, um, us, dw, dm, ds,
    out_ref,
    fg_ref,
    fu_ref,
    fd_ref,
    win,
    fresh,
    got0,
    got1,
    got2,
    arr,
    agx,
    agm,
    pbuf,
    prow,
    orow,
    yown,
    yoth,
    yin,
    yret,
    rret,
    part,
    rs_out,
    rs_in,
    load_sem,
    self_sem,
    self2_sem,
    send1,
    recv1,
    send2,
    recv2,
    ring_send,
    ring_recv,
    meta_send,
    meta_recv,
    plane_send,
    plane_recv,
    plane_self,
    x_send,
    x_recv,
    y_send,
    y_recv,
    ret_send,
    ret_recv,
    ret_self,
    rs_send,
    rs_recv,
):
    a = lax.axis_index("dp")
    e = lax.axis_index("expert")
    core = a % 2
    zlo = e % ZL
    xy = e // ZL
    z = (a // 2) * ZL + zlo

    def line(position):
        return ((position // ZL) * 2 + core, xy * ZL + position % ZL)

    def plane(spot):
        return (a, spot * ZL + zlo)

    partner_core = ((a // 2) * 2 + 1 - core, e)

    barrier = pltpu.get_barrier_semaphore()

    def greet_group(i, _):
        pl.semaphore_signal(barrier, inc=1, device_id=(a, (e + i) % GROUP), device_id_type=MESH)
        return _

    lax.fori_loop(1, GROUP, greet_group, 0)

    def greet_line(i, _):
        far = (1 - a // 2) * ZL + i
        pl.semaphore_signal(barrier, inc=1, device_id=line(far), device_id_type=MESH)
        return _

    lax.fori_loop(0, ZL, greet_line, 0)
    pl.semaphore_signal(barrier, inc=1, device_id=partner_core, device_id_type=MESH)

    sources = (gw, gm, gs, uw, um, us, dw, dm, ds)
    loads = [
        pltpu.make_async_copy(sources[i], win.at[i], load_sem.at[i]) for i in range(9)
    ]
    for copy in loads:
        copy.start()
    agx[z] = ffn_ref[...]
    agm[z] = meta_ref[...]
    pl.semaphore_wait(barrier, GROUP + ZL)

    def ring(step, way):
        if way == 0:
            block = (z - step + 1 + ZN) % ZN
            target = line((z + 1) % ZN)
        else:
            block = (z + step - 1) % ZN
            target = line((z - 1 + ZN) % ZN)
        if step == HALF:
            view = agx.at[block, pl.ds(way * (TOK // 2), TOK // 2)]
        else:
            view = agx.at[block]
        return pltpu.make_async_remote_copy(
            src_ref=view,
            dst_ref=view,
            send_sem=ring_send.at[way, step - 1],
            recv_sem=ring_recv.at[way, step - 1],
            device_id=target,
            device_id_type=MESH,
        )

    def ring_arrival(step, way):
        if way == 0:
            block = (z - step + ZN) % ZN
        else:
            block = (z + step) % ZN
        if step == HALF:
            view = agx.at[block, pl.ds(way * (TOK // 2), TOK // 2)]
        else:
            view = agx.at[block]
        pltpu.make_async_copy(view, view, ring_recv.at[way, step - 1]).wait()

    for way in range(2):
        ring(1, way).start()

    def meta_copy(i):
        return pltpu.make_async_remote_copy(
            src_ref=meta_ref,
            dst_ref=agm.at[z],
            send_sem=meta_send,
            recv_sem=meta_recv,
            device_id=line((z + i) % ZN),
            device_id_type=MESH,
        )

    def send_meta(i, _):
        meta_copy(i).start()
        return _

    lax.fori_loop(1, ZN, send_meta, 0)

    gots = (got0, got1, got2)
    outs = (fg_ref, fu_ref, fd_ref)

    def refresh_chunk(k):
        for i in range(3):
            loads[3 * k + i].wait()

        def tile(i, _):
            rows = pl.ds(pl.multiple_of(i * 32, 32), 32)
            fresh[k, rows, :] = refresh(
                win[3 * k, rows, :], win[3 * k + 1, rows, :], win[3 * k + 2, rows, :]
            )
            return _

        lax.fori_loop(0, D // 32, tile, 0)

    def piece_target(i):
        other = ((xy // 4 + i // 16) % 4) * 16 + ((xy % 4 + (i // 4) % 4) % 4) * 4 + (zlo + i % 4) % 4
        return other

    def scatter_chunk(k):
        def send(i, _):
            other = piece_target(i)
            pltpu.make_async_remote_copy(
                src_ref=fresh.at[k, pl.ds(pl.multiple_of(other * PIECE, PIECE), PIECE)],
                dst_ref=gots[k].at[e],
                send_sem=send1.at[k],
                recv_sem=recv1.at[k],
                device_id=(a, other),
                device_id_type=MESH,
            ).start()
            return _

        pltpu.make_async_copy(
            fresh.at[k, pl.ds(pl.multiple_of(e * PIECE, PIECE), PIECE)], gots[k].at[e], self_sem.at[k]
        ).start()
        lax.fori_loop(1, GROUP, send, 0)

    def regroup_chunk(k):
        got = gots[k]
        bulk = got.at[pl.ds(0, GROUP - 1)]
        pltpu.make_async_copy(bulk, bulk, recv1.at[k]).wait()
        pltpu.make_async_copy(
            fresh.at[k, pl.ds(pl.multiple_of(e * PIECE, PIECE), PIECE)], got.at[e], self_sem.at[k]
        ).wait()

        def pick(i, _):
            arr[k, i] = got[partner_ref[i]]
            return _

        lax.fori_loop(0, GROUP, pick, 0)

        mine = outs[k].at[pl.ds(pl.multiple_of(e * PIECE, PIECE), PIECE)]
        pltpu.make_async_copy(arr.at[k, e], mine, self2_sem.at[k]).start()

        def send(i, _):
            other = piece_target(i)
            pltpu.make_async_remote_copy(
                src_ref=arr.at[k, other],
                dst_ref=mine,
                send_sem=send2.at[k],
                recv_sem=recv2.at[k],
                device_id=(a, other),
                device_id_type=MESH,
            ).start()
            return _

        lax.fori_loop(1, GROUP, send, 0)

    def pair_blocks(p):
        first = (z - (p + 1) % HALF + ZN) % ZN
        second = (z + 1 + p) % ZN
        return first, second

    def choices(p):
        first, second = pair_blocks(p)
        ma, mb = agm[first], agm[second]
        row = lax.broadcasted_iota(jnp.int32, (ROWS, 1), 0)
        column = lax.broadcasted_iota(jnp.int32, (1, 2 * TOK), 1)
        code = (zlo * (XY * SLOTS) + (row // (2 * SLOTS)) * SLOTS + row % SLOTS).astype(jnp.float32)
        same = (row // SLOTS) % 2 == column // TOK
        both = jnp.concatenate([ma, mb], axis=1)
        hit0 = (both[0:1] == code) & same
        hit1 = (both[1:2] == code) & same
        return hit0, hit1, both

    def dispatch(p):
        first, second = pair_blocks(p)
        hit0, hit1, _ = choices(p)
        select = jnp.where(hit0 | hit1, 1.0, 0.0).astype(jnp.bfloat16)
        rows = jnp.dot(select[:, :TOK], agx[first], preferred_element_type=jnp.float32)
        rows = rows + jnp.dot(select[:, TOK:], agx[second], preferred_element_type=jnp.float32)
        pbuf[p] = rows.astype(jnp.bfloat16)
        mine = prow.at[p, pl.ds(pl.multiple_of(xy * 2 * SLOTS, 2 * SLOTS), 2 * SLOTS)]
        pltpu.make_async_copy(
            pbuf.at[p, pl.ds(pl.multiple_of(xy * 2 * SLOTS, 2 * SLOTS), 2 * SLOTS)], mine, plane_self.at[p]
        ).start()

        def send(i, _):
            spot = (xy + i) % XY
            pltpu.make_async_remote_copy(
                src_ref=pbuf.at[p, pl.ds(pl.multiple_of(spot * 2 * SLOTS, 2 * SLOTS), 2 * SLOTS)],
                dst_ref=mine,
                send_sem=plane_send.at[p],
                recv_sem=plane_recv.at[p],
                device_id=plane(spot),
                device_id_type=MESH,
            ).start()
            return _

        lax.fori_loop(1, XY, send, 0)

    BULK = pl.ds(0, ROWS - 2 * SLOTS)
    OWN = pl.ds(pl.multiple_of(xy * 2 * SLOTS, 2 * SLOTS), 2 * SLOTS)

    refresh_chunk(0)
    scatter_chunk(0)
    for p in range(HALF):
        for way in range(2):
            ring_arrival(p + 1, way)
        if p + 2 <= HALF:
            for way in range(2):
                ring(p + 2, way).start()
        if p == 0:
            line_meta = agm.at[pl.ds(0, ZN - 1)]
            pltpu.make_async_copy(line_meta, line_meta, meta_recv).wait()
        dispatch(p)
        if p + 1 < 3:
            refresh_chunk(p + 1)
            scatter_chunk(p + 1)

    regroup_chunk(0)

    def expert_part(rows):
        gate_pre = jnp.dot(rows, fresh[0], preferred_element_type=jnp.float32) * D ** (-0.5)
        up_pre = jnp.dot(rows, fresh[1], preferred_element_type=jnp.float32) * D ** (-0.5)
        hidden = (silu(gate_pre) * up_pre).astype(jnp.bfloat16)
        return lax.dot_general(
            hidden, fresh[2], (((1,), (1,)), ((), ())), preferred_element_type=jnp.float32
        ) * FF ** (-0.5)

    def exchange(src, dst, p, send, recv):
        return pltpu.make_async_remote_copy(
            src_ref=src.at[p],
            dst_ref=dst.at[p],
            send_sem=send.at[p],
            recv_sem=recv.at[p],
            device_id=partner_core,
            device_id_type=MESH,
        )

    def settle(p):
        exchange(yoth, yin, p, y_send, y_recv).wait_recv()
        yret[p] = (yown[p] + yin[p].astype(jnp.float32)).astype(jnp.bfloat16)
        pltpu.make_async_copy(yret.at[p, OWN], rret.at[p, OWN], ret_self.at[p]).start()

        def send(i, _):
            spot = (xy + i) % XY
            pltpu.make_async_remote_copy(
                src_ref=yret.at[p, pl.ds(pl.multiple_of(spot * 2 * SLOTS, 2 * SLOTS), 2 * SLOTS)],
                dst_ref=rret.at[p, OWN],
                send_sem=ret_send.at[p],
                recv_sem=ret_recv.at[p],
                device_id=plane(spot),
                device_id_type=MESH,
            ).start()
            return _

        lax.fori_loop(1, XY, send, 0)

    def experts(p, _):
        bulk = prow.at[p, BULK]
        pltpu.make_async_copy(bulk, bulk, plane_recv.at[p]).wait()
        pltpu.make_async_copy(pbuf.at[p, OWN], prow.at[p, OWN], plane_self.at[p]).wait()
        exchange(prow, orow, p, x_send, x_recv).start()
        yown[p] = expert_part(prow[p])
        exchange(prow, orow, p, x_send, x_recv).wait_recv()
        yoth[p] = expert_part(orow[p]).astype(jnp.bfloat16)
        exchange(yoth, yin, p, y_send, y_recv).start()

        @pl.when(p > 0)
        def _settle():
            settle(p - 1)

        return _

    lax.fori_loop(0, HALF, experts, 0)
    settle(HALF - 1)
    regroup_chunk(1)

    def combine(p, _):
        bulk = rret.at[p, BULK]
        pltpu.make_async_copy(bulk, bulk, ret_recv.at[p]).wait()
        pltpu.make_async_copy(yret.at[p, OWN], rret.at[p, OWN], ret_self.at[p]).wait()
        first, second = pair_blocks(p)
        hit0, hit1, both = choices(p)
        weights = jnp.where(hit0, both[2:3], 0.0) + jnp.where(hit1, both[3:4], 0.0)
        weights = weights.T.astype(jnp.bfloat16)
        total = jnp.dot(weights, rret[p], preferred_element_type=jnp.float32)
        part[first] = total[:TOK]
        part[second] = total[TOK:]
        return _

    lax.fori_loop(0, HALF, combine, 0)

    def rs_view(ref, step, way):
        if step == 1:
            return ref.at[way, step - 1, pl.ds(way * (TOK // 2), TOK // 2)]
        return ref.at[way, step - 1]

    def rs(step, way):
        target = line((z + 1) % ZN) if way == 0 else line((z - 1 + ZN) % ZN)
        return pltpu.make_async_remote_copy(
            src_ref=rs_view(rs_out, step, way),
            dst_ref=rs_view(rs_in, step, way),
            send_sem=rs_send.at[way, step - 1],
            recv_sem=rs_recv.at[way, step - 1],
            device_id=target,
            device_id_type=MESH,
        )

    for step in range(1, HALF + 1):
        for way in range(2):
            distance = HALF + 1 - step
            owner = (z + distance) % ZN if way == 0 else (z - distance + ZN) % ZN
            half = pl.ds(way * (TOK // 2), TOK // 2)
            other_half = pl.ds((1 - way) * (TOK // 2), TOK // 2)
            if step > 1:
                rs(step - 1, way).wait_recv()
            if step == 1:
                rs_out[way, 0, half, :] = part[owner, half, :].astype(jnp.bfloat16)
            elif step == 2:
                rs_out[way, 1, half, :] = (
                    part[owner, half, :] + rs_in[way, 0, half, :].astype(jnp.float32)
                ).astype(jnp.bfloat16)
                rs_out[way, 1, other_half, :] = part[owner, other_half, :].astype(jnp.bfloat16)
            else:
                rs_out[way, step - 1] = (
                    part[owner] + rs_in[way, step - 2].astype(jnp.float32)
                ).astype(jnp.bfloat16)
            rs(step, way).start()
        if step == 1:
            regroup_chunk(2)
    for way in range(2):
        rs(HALF, way).wait_recv()
    moe = (
        part[z]
        + rs_in[0, HALF - 1].astype(jnp.float32)
        + rs_in[1, HALF - 1].astype(jnp.float32)
    )
    out_ref[...] = (mixed_ref[...].astype(jnp.float32) + 0.5 * moe).astype(jnp.bfloat16)

    for way in range(2):
        for step in range(1, HALF + 1):
            ring(step, way).wait_send()
            rs(step, way).wait_send()
    for k in range(3):
        bulk = arr.at[k, pl.ds(0, GROUP - 1)]
        pltpu.make_async_copy(bulk, bulk, send1.at[k]).wait()
        pltpu.make_async_copy(bulk, bulk, send2.at[k]).wait()
        landed = outs[k].at[pl.ds(0, D - PIECE)]
        pltpu.make_async_copy(landed, landed, recv2.at[k]).wait()
        mine = outs[k].at[pl.ds(pl.multiple_of(e * PIECE, PIECE), PIECE)]
        pltpu.make_async_copy(arr.at[k, e], mine, self2_sem.at[k]).wait()
    sent_meta = agm.at[pl.ds(0, ZN - 1)]
    pltpu.make_async_copy(sent_meta, sent_meta, meta_send).wait()
    for p in range(HALF):
        bulk = pbuf.at[p, BULK]
        pltpu.make_async_copy(bulk, bulk, plane_send.at[p]).wait()
        bulk = yret.at[p, BULK]
        pltpu.make_async_copy(bulk, bulk, ret_send.at[p]).wait()
        exchange(prow, orow, p, x_send, x_recv).wait_send()
        exchange(yoth, yin, p, y_send, y_recv).wait_send()


def communicate(partner, ffn_in, mixed_rows, meta, weights):
    bf16, f32 = jnp.bfloat16, jnp.float32
    dma = pltpu.SemaphoreType.DMA
    vmem = pl.BlockSpec(memory_space=pltpu.VMEM)
    anyspace = pl.BlockSpec(memory_space=pl.ANY)
    moved = jax.ShapeDtypeStruct((D, FLOC), bf16)
    return pl.pallas_call(
        kernel,
        out_shape=(jax.ShapeDtypeStruct((TOK, D), bf16), moved, moved, moved),
        in_specs=[pl.BlockSpec(memory_space=pltpu.SMEM), vmem, vmem, vmem] + [anyspace] * 9,
        out_specs=(vmem, anyspace, anyspace, anyspace),
        scratch_shapes=[
            pltpu.VMEM((9, D, FLOC), bf16),
            pltpu.VMEM((3, D, FLOC), bf16),
            pltpu.VMEM((GROUP, PIECE, FLOC), bf16),
            pltpu.VMEM((GROUP, PIECE, FLOC), bf16),
            pltpu.VMEM((GROUP, PIECE, FLOC), bf16),
            pltpu.VMEM((3, GROUP, PIECE, FLOC), bf16),
            pltpu.VMEM((ZN, TOK, D), bf16),
            pltpu.VMEM((ZN, 8, TOK), f32),
            pltpu.VMEM((HALF, ROWS, D), bf16),
            pltpu.VMEM((HALF, ROWS, D), bf16),
            pltpu.VMEM((HALF, ROWS, D), bf16),
            pltpu.VMEM((HALF, ROWS, D), f32),
            pltpu.VMEM((HALF, ROWS, D), bf16),
            pltpu.VMEM((HALF, ROWS, D), bf16),
            pltpu.VMEM((HALF, ROWS, D), bf16),
            pltpu.VMEM((HALF, ROWS, D), bf16),
            pltpu.VMEM((ZN, TOK, D), f32),
            pltpu.VMEM((2, HALF, TOK, D), bf16),
            pltpu.VMEM((2, HALF, TOK, D), bf16),
            dma((9,)),
            dma((3,)),
            dma((3,)),
            dma((3,)),
            dma((3,)),
            dma((3,)),
            dma((3,)),
            dma((2, HALF)),
            dma((2, HALF)),
            dma,
            dma,
            dma((HALF,)),
            dma((HALF,)),
            dma((HALF,)),
            dma((HALF,)),
            dma((HALF,)),
            dma((HALF,)),
            dma((HALF,)),
            dma((HALF,)),
            dma((HALF,)),
            dma((HALF,)),
            dma((2, HALF)),
            dma((2, HALF)),
        ],
        compiler_params=pltpu.CompilerParams(
            collective_id=0, has_side_effects=True, vmem_limit_bytes=64 * 1024 * 1024 - 65536
        ),
    )(partner, ffn_in, mixed_rows, meta, *weights)


def shards(
    frames,
    lengths,
    expert_ids,
    capacity,
    resident,
    partner,
    conv_gain,
    conv_kernel,
    conv_bias,
    ffn_gain,
    router,
    gate_weight,
    up_weight,
    down_weight,
    gate_mean_grad,
    gate_mean_square,
    up_mean_grad,
    up_mean_square,
    down_mean_grad,
    down_mean_square,
):
    devices = lax.axis_size("expert")
    position = lax.axis_index("expert")
    frame_count = frames.shape[0]
    margin = (K - 1) // 2
    span_total = devices * frame_count

    start_pos = position * frame_count
    seq_length = lengths[0]
    offsets = start_pos + jnp.arange(frame_count, dtype=jnp.int32)
    live_rows = (offsets < seq_length).astype(jnp.float32)[:, None]
    inputs_f = frames.astype(jnp.float32)
    normed = (layer_norm(inputs_f, conv_gain) * live_rows).astype(jnp.bfloat16)
    padded = extended(normed, (("expert", 0),), margin)
    wide_pos = start_pos - margin + jnp.arange(frame_count + 2 * margin, dtype=jnp.int32)
    same_utterance = ((wide_pos >= 0) & (wide_pos < span_total)).astype(jnp.float32)[:, None]
    widened = padded.astype(jnp.float32) * same_utterance
    conv_sum = jnp.zeros((frame_count, frames.shape[1]), jnp.float32)
    for tap_index in range(K):
        conv_sum = conv_sum + conv_kernel[tap_index] * widened[tap_index : tap_index + frame_count]
    mixed_rows = (inputs_f + live_rows * jax.nn.silu(conv_sum + conv_bias)).astype(jnp.bfloat16)
    ffn_in = layer_norm(mixed_rows.astype(jnp.float32), ffn_gain).astype(jnp.bfloat16)
    logits = jnp.dot(ffn_in, router, preferred_element_type=jnp.float32)
    expert_iota = jnp.arange(router.shape[1], dtype=jnp.int32)
    picked = expert_ids[:, :, None] == expert_iota[None, None, :]
    chosen = jnp.sum(jnp.where(picked, logits[:, None, :], 0.0), axis=-1)
    scores = jax.nn.sigmoid(chosen)
    gate_values = (scores / jnp.sum(scores, axis=-1, keepdims=True)).astype(jnp.bfloat16)
    old_slot = jnp.sum(
        jnp.where(resident[None, :] == expert_iota[:, None], expert_iota[None, :], 0), axis=1
    )
    place = (old_slot % ZL) * (XY * SLOTS) + (old_slot // ZL) * SLOTS
    flat_ids = expert_ids.reshape(-1)
    onehot = (flat_ids[:, None] == expert_iota[None, :]).astype(jnp.int32)
    earlier = jnp.cumsum(onehot, axis=0) - onehot
    rank_in_block = jnp.sum(earlier * onehot, axis=1)
    slot_limit = jnp.sum(onehot * capacity[None, :], axis=1)
    dest = jnp.sum(onehot * place[None, :], axis=1)
    code = jnp.where(rank_in_block < slot_limit, dest + rank_in_block, -1).reshape(frame_count, 2)
    meta = jnp.concatenate(
        [
            code.astype(jnp.float32).T,
            gate_values.astype(jnp.float32).T,
            jnp.zeros((4, frame_count), jnp.float32),
        ],
        axis=0,
    )
    block_out, fresh_gate, fresh_up, fresh_down = communicate(
        partner,
        ffn_in,
        mixed_rows,
        meta,
        (
            gate_weight[0], gate_mean_grad[0], gate_mean_square[0],
            up_weight[0], up_mean_grad[0], up_mean_square[0],
            down_weight[0], down_mean_grad[0], down_mean_square[0],
        ),
    )
    return (block_out, fresh_gate[None], fresh_up[None], fresh_down[None])


def solution(mesh):
    placed = (
        P(("dp", "expert"), None),
        P("dp"),
        P(("dp", "expert"), None),
        P(),
        P(),
        P(),
        P(),
        P(),
        P(),
        P(),
        P(),
        P("expert", None, "dp"),
        P("expert", None, "dp"),
        P("expert", None, "dp"),
        P("expert", None, "dp"),
        P("expert", None, "dp"),
        P("expert", None, "dp"),
        P("expert", None, "dp"),
        P("expert", None, "dp"),
        P("expert", None, "dp"),
    )
    return jax.shard_map(
        shards,
        mesh=mesh,
        in_specs=placed,
        out_specs=(
            P(("dp", "expert"), None),
            P("expert", None, "dp"),
            P("expert", None, "dp"),
            P("expert", None, "dp"),
        ),
        check_vma=False,
    )
```

time: 487 us -> 234 us (0.48); the launches traced: 478 us -> 230 us
  waiting for transfers between devices: 224 us -> 0.01 us
  Pallas kernels: 0 us -> 198 us
  other arithmetic: 72.5 us -> 7.53 us
  starting transfers between devices: 73.2 us -> 11 us
  local copies, waits for them, and re-layouts: 69.2 us -> 11.9 us
  matrix products: 22.7 us -> 0.2 us
  between operations: 15.9 us -> 1.6 us
    pallas_call x0 -> x1, Pallas kernels: none -> 198 us  [communicate(): pl.pallas_call(kernel, out_shape=(jax.ShapeDtypeStruct((TOK, D), bf16), m...]
    all_to_all x8 -> x0, waiting for transfers between devices: 145 us -> none  [the longest x1 65.4 us: shards(): lax.all_to_all(arranged[0], 'expert', split_axis=0, concat_axis=0, tiled=...]
    reduce_scatter x1 -> x0, waiting for transfers between devices: 78.7 us -> none  [shards(): lax.psum_scatter(expert_part(everyone, gate_local, up_local, down_local)....]
    all_to_all x8 -> x0, starting transfers between devices: 62.3 us -> none  [the longest x1 12.4 us: shards(): lax.all_to_all(flatten_rows(local_gate), 'expert', split_axis=0, concat_a...]
    all_to_all x10 -> x0, other arithmetic: 54.6 us -> none  [the longest x3 12.8 us: shards(): lax.all_to_all(arranged[1], 'expert', split_axis=0, concat_axis=0, tiled=...]
    unnamed x86 -> x31, local copies, waits for them, and re-layouts: 43 us -> 11 us
    dot_general x4 -> x0, matrix products: 21.8 us -> none  [the longest x1 11.2 us: expert_part(): lax.dot_general(hidden, down_block, (((1,), (1,)), ((), ())), preferred_e...]
    convert_element_type x4 -> x3, other arithmetic: 9.76 us -> 0.24 us  [the longest x1 0.22 us: shards(): layer_norm(mixed_rows.astype(jnp.float32), ffn_gain).astype(jnp.bfloat16)]
  transfers between devices with their start and end apart: 12 -> 2, of which waited for: 8 -> 0; matrix products, arithmetic and copies ran while one was open for 26% -> 1% of each run, Pallas kernels for 0% -> 0%
where the time goes in v1:
time: 234 us; the launch traced here: 230 us
  Pallas kernels  198 us (85%)
  local copies, waits for them, and re-layouts  11.9 us (5%)
  starting transfers between devices  11 us (5%)
  other arithmetic  7.53 us (3%)
    pallas_call x1, Pallas kernels, communicate(): pl.pallas_call(kernel, out_shape=(jax.ShapeDtypeStruct((TOK, D), bf16), m...  198 us
    unnamed x31, local copies, waits for them, and re-layouts  11 us
    ppermute x1, starting transfers between devices, extended(): lax.ppermute(head, axis, [((i + 1) % count, i) for i in range(ends)])  7.05 us
    reduce_sum x2, other arithmetic, layer_norm(): centred = values - jnp.mean(values, axis=-1, keepdims=True)  4.86 us
  transfers between devices with their start and end apart: 2, of which 0 were waited for; matrix products, arithmetic and copies ran while one was open for 1% of the time, Pallas kernels for 0%

profile of v1, /device:TPU:2, one launch (start us, length us, event | category | flops | bytes accessed | tf_op | source)
XLA Modules:
  0.0 230.4 jit_solution(3330628767729302238)
XLA Ops:
  0.6 0.0 copy-start
  1.3 1.1 convert_reduce_fusion
  2.4 0.0 copy-done
  2.4 0.2 fusion.4
  2.6 0.0 copy-start.7
  2.7 0.7 copy-done.7
  3.3 0.2 fusion.7
  3.6 0.0 copy-start.10
  3.6 0.0 copy-start.6
  3.6 4.0 %collective-permute-start = (bf16[15,1024]{1,0:T(8,128)(2,1)S(1)}, bf16[15,1024]{1,0:T(8,128)(2,1)S(1)}, u32[]{:S(2)}, u32[]{:S(2)}) collective-permute-start(bf16[15,1024]{1,0:T(8,128)(2,1)S(1)} %get-tuple-element.17), channel_id=1, source_target_pairs={{0,1},{1,2},{2,3},{3,4},{4,5},{5,6},{6,7},{7,8},{8,9},{9,10},{10,1... | collective-permute-start | bytes 92168 | tf_op jit(solution)/shard_map/ppermute | solution.py:40
  7.6 7.0 %collective-permute-start.1 = (bf16[15,1024]{1,0:T(8,128)(2,1)S(1)}, bf16[15,1024]{1,0:T(8,128)(2,1)S(1)}, u32[]{:S(2)}, u32[]{:S(2)}) collective-permute-start(bf16[15,1024]{1,0:T(8,128)(2,1)S(1)} %get-tuple-element.18), channel_id=1, source_target_pairs={{1,0},{2,1},{3,2},{4,3},{5,4},{6,5},{7,6},{8,7},{9,8},{10,9},{11,1... | collective-permute-start | bytes 92168 | tf_op jit(solution)/shard_map/ppermute | solution.py:42
  14.6 0.0 copy-done.10
  14.6 0.1 copy.32
  14.7 0.1 eq.57
  14.9 0.1 eq.53
  15.0 0.0 copy-done.6
  15.1 0.1 fusion.53
  15.2 0.0 copy-start.12
  15.2 0.6 copy-done.12
  15.8 0.1 select_reduce_fusion.3
  16.0 0.6 reduce-window.6
  16.6 0.2 slice_reduce_fusion
  16.8 0.0 copy-start.11
  16.8 0.7 copy-done.11
  17.5 0.1 select_reduce_fusion.1
  17.6 0.1 convert_element_type.64
  17.7 0.1 copy.35
  17.8 0.1 pad.2.clone
  17.9 0.0 collective-permute-done
  17.9 0.0 collective-permute-done.1
  17.9 0.1 convert_multiply_fusion
  18.0 0.0 copy-start.8
  18.0 0.7 copy-done.8
  18.7 3.8 %convert_reduce_fusion.1 = (f32[128]{0:T(128)S(1)}, bf16[128,1024]{1,0:T(8,128)(2,1)S(1)}) fusion(f32[1024]{0:T(1024)S(1)} %copy-done.8, f32[158,1024]{1,0:T(8,128)S(1)} %convert_multiply_fusion, f32[1024]{0:T(1024)S(1)} %bitcast.91, f32[1024]{0:T(1024)S(1)} %bitcast.92, f32[1024]{0:T(1024)S(1)} %bitcast.94, f32[1024]{0:T(1024)S(1)} %bitcast.95, ...), kind=kLoop, calls=%fused_computation.4 | loop fusion | flops 9437056 | bytes 16909312 | tf_op jit(solution)/shard_map/reduce_sum | solution.py:50
  22.5 0.0 copy-start.1
  22.5 0.0 copy-start.9
  22.6 0.2 fusion.8
  22.8 0.5 copy-done.9
  23.3 0.0 copy-start.5
  23.3 0.2 fusion.10.ffn_ref
  23.5 0.0 copy-done.1
  23.5 0.7 copy-done.5
  24.2 0.0 copy-start.2
  24.2 0.2 fusion.55
  24.4 0.5 copy-done.2
  25.0 0.7 maximum_maximum_fusion.meta_ref
  25.6 198.2 %shard_map.219 = (bf16[128,1024]{1,0:T(8,128)(2,1)}, bf16[1024,512]{1,0:T(8,128)(2,1)}, bf16[1024,512]{1,0:T(8,128)(2,1)}, bf16[1024,512]{1,0:T(8,128)(2,1)}) custom-call(s32[64]{0:T(128)} %partner_ref.1, bf16[128,1024]{1,0:T(8,128)(2,1)} %copy-done.2, bf16[128,1024]{1,0:T(8,128)(2,1)} %copy-done.1, f32[8,128]{1,0:T(8,128)} %maximum_maximum_fusion.meta_ref, ...), custom_call_target="tpu_custom_call" | custom-call | tf_op jit(solution)/shard_map/pallas_call | solution.py:493
  223.8 1.7 copy.43
  225.5 0.0 copy-start.4
  225.5 2.4 %copy.44 = bf16[1,1024,512]{2,1,0:T(8,128)(2,1)} copy(bf16[1,1024,512]{2,1,0:T(8,128)(2,1)} %bitcast.80) | data formatting | bytes 2097152
  227.8 0.0 copy-done.4
  227.8 0.0 copy-start.3
  227.8 1.0 copy.45
  228.8 0.6 copy-done.3
  229.4 1.0 copy.46
  (17 shorter events, 0.2 us)
Async XLA Ops:
  0.6 1.8 copy-start
  2.6 0.7 copy-start.7
  3.6 11.1 %copy-start.10 = (s32[128,2]{0,1:T(2,128)S(1)}, s32[128,2]{0,1:T(2,128)}, u32[]{:S(2)}) copy-start(s32[128,2]{0,1:T(2,128)} %param.22) | copy-start | bytes 3076
  3.6 11.4 %copy-start.6 = (f32[31,1024]{1,0:T(8,128)S(1)}, f32[31,1024]{1,0:T(8,128)}, u32[]{:S(2)}) copy-start(f32[31,1024]{1,0:T(8,128)} %param.27) | copy-start | bytes 380932
  3.6 14.3 %collective-permute-start = (bf16[15,1024]{1,0:T(8,128)(2,1)S(1)}, bf16[15,1024]{1,0:T(8,128)(2,1)S(1)}, u32[]{:S(2)}, u32[]{:S(2)}) collective-permute-start(bf16[15,1024]{1,0:T(8,128)(2,1)S(1)} %get-tuple-element.17), channel_id=1, source_target_pairs={{0,1},{1,2},{2,3},{3,4},{4,5},{5,6},{6,7},{7,8},{8,9},{9,10},{10,1... | collective-permute-start | bytes 92168 | tf_op jit(solution)/shard_map/ppermute | solution.py:40
  7.6 10.3 %collective-permute-start.1 = (bf16[15,1024]{1,0:T(8,128)(2,1)S(1)}, bf16[15,1024]{1,0:T(8,128)(2,1)S(1)}, u32[]{:S(2)}, u32[]{:S(2)}) collective-permute-start(bf16[15,1024]{1,0:T(8,128)(2,1)S(1)} %get-tuple-element.18), channel_id=1, source_target_pairs={{1,0},{2,1},{3,2},{4,3},{5,4},{6,5},{7,6},{8,7},{9,8},{10,9},{11,1... | collective-permute-start | bytes 92168 | tf_op jit(solution)/shard_map/ppermute | solution.py:42
  15.2 0.7 copy-start.12
  16.8 0.7 copy-start.11
  18.0 0.7 copy-start.8
  22.5 1.0 copy-start.1
  22.5 0.7 copy-start.9
  23.3 0.9 copy-start.5
  24.2 0.7 copy-start.2
  225.5 2.4 %copy-start.4 = (bf16[1024,512]{1,0:T(8,128)(2,1)S(1)}, bf16[1024,512]{1,0:T(8,128)(2,1)}, u32[]{:S(2)}) copy-start(bf16[1024,512]{1,0:T(8,128)(2,1)} %get-tuple-element.10) | copy-start | bytes 3145732
  227.8 1.6 copy-start.3

commit v2 on v1

v2 whole, which is shorter than its diff:
```python
import functools

import jax
import jax.numpy as jnp
from jax import lax
from jax.experimental import pallas as pl
from jax.experimental.pallas import tpu as pltpu
from jax.sharding import PartitionSpec as P

D = 1024
FF = 2048
K = 31


LEARNING_RATE = 0.1
ADAM_EPSILON = 1e-08
NORM_EPSILON = 1e-05

MESH = pl.DeviceIdType.MESH
XY = 16
ZL = 4
ZN = 8
HALF = ZN // 2
GROUP = XY * ZL
SLOTS = 8
TOK = 128
FLOC = 512
ROWS = XY * 2 * SLOTS
SIDE = GROUP // 2
WIDE = 48
NARROW = 16
CHUNKS = 6
CCOL = FLOC // 2
MARGIN = (K - 1) // 2
EDGE = 16
TILE = 32
CAPS = (16, 20, SIDE)


def layer_norm(values, gain_row):
    centred = values - jnp.mean(values, axis=-1, keepdims=True)
    variance = jnp.mean(centred * centred, axis=-1, keepdims=True)
    return centred * lax.rsqrt(variance + NORM_EPSILON) * gain_row


def refresh(weight, first_moment, second_moment):
    step_size = (
        LEARNING_RATE
        * first_moment.astype(jnp.float32)
        / (jnp.sqrt(second_moment.astype(jnp.float32)) + ADAM_EPSILON)
    )
    return (weight.astype(jnp.float32) - step_size).astype(jnp.bfloat16)


def silu(value):
    return value / (1.0 + jnp.exp(-value))


def kernel(
    cap,
    send_list_ref,
    source_ref,
    length_ref,
    frames_ref,
    ids_ref,
    table_ref,
    conv_gain_ref,
    taps_ref,
    bias_ref,
    ffn_gain_ref,
    router_ref,
    gw, gm, gs, uw, um, us, dw, dm, ds,
    out_ref,
    fg_ref,
    fu_ref,
    fd_ref,
    win,
    fresh,
    wide,
    normed,
    halo,
    mixed,
    meta_ref,
    got0, got1, got2, got3, got4, got5,
    cs0, cs1, cs2, cs3, cs4, cs5,
    cr0, cr1, cr2, cr3, cr4, cr5,
    arr,
    agx,
    agm,
    pbuf,
    xrow,
    yown,
    yoth,
    yin,
    yret,
    rret,
    part,
    rs_out,
    rs_in,
    halo_send,
    halo_recv,
    load_sem,
    self_sem,
    self2_sem,
    send1,
    recv1,
    sendx,
    recvx,
    send2,
    recv2,
    ring_send,
    ring_recv,
    meta_send,
    meta_recv,
    plane_send,
    plane_recv,
    plane_self,
    x_send,
    x_recv,
    y_send,
    y_recv,
    ret_send,
    ret_recv,
    ret_self,
    rs_send,
    rs_recv,
):
    a = lax.axis_index("dp")
    e = lax.axis_index("expert")
    core = a % 2
    zlo = e % ZL
    xy = e // ZL
    z = (a // 2) * ZL + zlo
    side = zlo // 2
    inner = ((zlo + 1) // 2) % 2
    local = xy * 2 + zlo % 2
    wide_of = 1 + side
    narrow_of = 3 * side

    def line(position):
        return ((position // ZL) * 2 + core, xy * ZL + position % ZL)

    def plane(spot):
        return (a, spot * ZL + zlo)

    partner_core = ((a // 2) * 2 + 1 - core, e)

    barrier = pltpu.get_barrier_semaphore()

    def greet_group(i, _):
        pl.semaphore_signal(barrier, inc=1, device_id=(a, (e + i) % GROUP), device_id_type=MESH)
        return _

    lax.fori_loop(1, GROUP, greet_group, 0)

    def greet_line(i, _):
        far = (1 - a // 2) * ZL + i
        pl.semaphore_signal(barrier, inc=1, device_id=line(far), device_id_type=MESH)
        return _

    lax.fori_loop(0, ZL, greet_line, 0)
    pl.semaphore_signal(barrier, inc=1, device_id=partner_core, device_id_type=MESH)

    sources = ((gw, gm, gs), (uw, um, us), (dw, dm, ds))

    def load(c, i):
        columns = pl.ds((c % 2) * CCOL, CCOL)
        return pltpu.make_async_copy(
            sources[c // 2][i].at[:, columns], win.at[c % 3, i], load_sem.at[c % 3, i]
        )

    for c in range(3):
        for i in range(3):
            load(c, i).start()

    length = length_ref[0]

    def first_norm(i, _):
        rows = pl.ds(pl.multiple_of(i * TILE, TILE), TILE)
        offset = e * TOK + i * TILE + lax.broadcasted_iota(jnp.int32, (TILE, 1), 0)
        live = jnp.where(offset < length, 1.0, 0.0)
        value = layer_norm(frames_ref[rows, :].astype(jnp.float32), conv_gain_ref[...]) * live
        value = value.astype(jnp.bfloat16)
        normed[rows, :] = value
        wide[pl.ds(pl.multiple_of(EDGE + i * TILE, EDGE), TILE), :] = value.astype(jnp.float32)
        return _

    lax.fori_loop(0, TOK // TILE, first_norm, 0)
    pl.semaphore_wait(barrier, GROUP + ZL)

    def edge(way):
        start = TOK - EDGE if way == 0 else 0
        neighbour = (e + 1) % GROUP if way == 0 else (e - 1 + GROUP) % GROUP
        return pltpu.make_async_remote_copy(
            src_ref=normed.at[pl.ds(start, EDGE)],
            dst_ref=halo.at[way],
            send_sem=halo_send.at[way],
            recv_sem=halo_recv.at[way],
            device_id=(a, neighbour),
            device_id_type=MESH,
        )

    for way in range(2):
        edge(way).start()

    def ring(step, way):
        if way == 0:
            block = (z - step + 1 + ZN) % ZN
            target = line((z + 1) % ZN)
        else:
            block = (z + step - 1) % ZN
            target = line((z - 1 + ZN) % ZN)
        if step == HALF:
            view = agx.at[block, pl.ds(way * (TOK // 2), TOK // 2)]
        else:
            view = agx.at[block]
        return pltpu.make_async_remote_copy(
            src_ref=view,
            dst_ref=view,
            send_sem=ring_send.at[way, step - 1],
            recv_sem=ring_recv.at[way, step - 1],
            device_id=target,
            device_id_type=MESH,
        )

    def ring_arrival(step, way):
        if way == 0:
            block = (z - step + ZN) % ZN
        else:
            block = (z + step) % ZN
        if step == HALF:
            view = agx.at[block, pl.ds(way * (TOK // 2), TOK // 2)]
        else:
            view = agx.at[block]
        pltpu.make_async_copy(view, view, ring_recv.at[way, step - 1]).wait()

    def meta_copy(i):
        return pltpu.make_async_remote_copy(
            src_ref=meta_ref,
            dst_ref=agm.at[z],
            send_sem=meta_send,
            recv_sem=meta_recv,
            device_id=line((z + i) % ZN),
            device_id_type=MESH,
        )

    def send_meta(i, _):
        meta_copy(i).start()
        return _

    gots = (got0, got1, got2, got3, got4, got5)
    crosses_out = (cs0, cs1, cs2, cs3, cs4, cs5)
    crosses_in = (cr0, cr1, cr2, cr3, cr4, cr5)
    outs = (fg_ref, fu_ref, fd_ref)

    def refresh_chunk(k):
        for i in range(3):
            load(k, i).wait()
        slot = k % 3

        def tile(i, _):
            rows = pl.ds(pl.multiple_of(i * 64, 64), 64)
            fresh[k // 2, rows, pl.ds((k % 2) * CCOL, CCOL)] = refresh(
                win[slot, 0, rows, :], win[slot, 1, rows, :], win[slot, 2, rows, :]
            )
            return _

        lax.fori_loop(0, D // 64, tile, 0)
        if k + 3 < CHUNKS:
            for i in range(3):
                load(k + 3, i).start()

    def fresh_rows(k, rows):
        return fresh.at[k // 2, rows, pl.ds((k % 2) * CCOL, CCOL)]

    def out_rows(k, rows):
        return outs[k // 2].at[rows, pl.ds((k % 2) * CCOL, CCOL)]

    def wide_rows(spot):
        return pl.ds(pl.multiple_of(spot * WIDE, NARROW), WIDE)

    def narrow_rows(spot):
        return pl.ds(pl.multiple_of(XY * WIDE + spot * NARROW, NARROW), NARROW)

    TALL = pl.ds(0, D - WIDE)
    TALLER = pl.ds(0, D - NARROW)
    PART = pl.ds(0, NARROW)
    MOST = pl.ds(0, SIDE - 1)

    def wait_bytes(view, sem):
        pltpu.make_async_copy(view, view, sem).wait()

    def scatter_chunk(k):
        got = gots[k]

        def to_wide(spot):
            return pltpu.make_async_remote_copy(
                src_ref=fresh_rows(k, wide_rows(spot)),
                dst_ref=got.at[local],
                send_sem=send1.at[k],
                recv_sem=recv1.at[k],
                device_id=(a, spot * ZL + wide_of),
                device_id_type=MESH,
            )

        def to_narrow(spot):
            return pltpu.make_async_remote_copy(
                src_ref=fresh_rows(k, narrow_rows(spot)),
                dst_ref=got.at[local, PART],
                send_sem=send1.at[k],
                recv_sem=recv1.at[k],
                device_id=(a, spot * ZL + narrow_of),
                device_id_type=MESH,
            )

        @pl.when(inner == 1)
        def _inner():
            pltpu.make_async_copy(fresh_rows(k, wide_rows(xy)), got.at[local], self_sem.at[k]).start()
            to_narrow(xy).start()

        @pl.when(inner == 0)
        def _outer():
            pltpu.make_async_copy(fresh_rows(k, narrow_rows(xy)), got.at[local, PART], self_sem.at[k]).start()
            to_wide(xy).start()

        def send(i, _):
            spot = ((xy // 4 + i // 4) % 4) * 4 + (xy + i) % 4
            to_wide(spot).start()
            to_narrow(spot).start()
            return _

        lax.fori_loop(1, XY, send, 0)

    def cross_copy(k, narrow):
        src, dst = crosses_out[k], crosses_in[k]
        return pltpu.make_async_remote_copy(
            src_ref=src.at[:, PART] if narrow else src,
            dst_ref=dst.at[:, PART] if narrow else dst,
            send_sem=sendx.at[k],
            recv_sem=recvx.at[k],
            device_id=(a, xy * ZL + ZL - 1 - zlo),
            device_id_type=MESH,
        )

    def cross_chunk(k):
        got, out = gots[k], crosses_out[k]

        @pl.when(inner == 1)
        def _inner():
            wait_bytes(got.at[MOST], recv1.at[k])
            pltpu.make_async_copy(fresh_rows(k, wide_rows(xy)), got.at[local], self_sem.at[k]).wait()

        @pl.when(inner == 0)
        def _outer():
            wait_bytes(got.at[MOST, PART], recv1.at[k])
            pltpu.make_async_copy(fresh_rows(k, narrow_rows(xy)), got.at[local, PART], self_sem.at[k]).wait()

        def pick(i, _):
            out[i] = got[send_list_ref[i]]
            return _

        lax.fori_loop(0, cap, pick, 0)

        @pl.when(inner == 1)
        def _send_inner():
            cross_copy(k, False).start()

        @pl.when(inner == 0)
        def _send_outer():
            cross_copy(k, True).start()

    def regroup_chunk(k):
        got, crossed = gots[k], crosses_in[k]

        @pl.when(inner == 1)
        def _inner():
            cross_copy(k, False).wait_recv()

        @pl.when(inner == 0)
        def _outer():
            cross_copy(k, True).wait_recv()

        def pick(i, _):
            index = source_ref[i]
            near = got[jnp.minimum(index, SIDE - 1)]
            far = crossed[jnp.maximum(index - SIDE, 0)]
            arr[k, i] = jnp.where(index < SIDE, near, far)
            return _

        lax.fori_loop(0, SIDE, pick, 0)

        def deliver(rows, part):
            def view(i):
                return arr.at[k, i, part] if part is not None else arr.at[k, i]

            pltpu.make_async_copy(view(local), out_rows(k, rows), self2_sem.at[k]).start()

            def send(i, _):
                spot = ((xy // 4 + i // 8) % 4) * 4 + (xy + i // 2) % 4
                end = (zlo + i) % 2
                pltpu.make_async_remote_copy(
                    src_ref=view(spot * 2 + end),
                    dst_ref=out_rows(k, rows),
                    send_sem=send2.at[k],
                    recv_sem=recv2.at[k],
                    device_id=(a, spot * ZL + side * 2 + end),
                    device_id_type=MESH,
                ).start()
                return _

            lax.fori_loop(1, SIDE, send, 0)

        @pl.when(inner == 1)
        def _deliver_inner():
            deliver(wide_rows(xy), None)

        @pl.when(inner == 0)
        def _deliver_outer():
            deliver(narrow_rows(xy), PART)

    def frame_module():
        for way in range(2):
            edge(way).wait_recv()
        has_left = jnp.where(e > 0, 1.0, 0.0)
        has_right = jnp.where(e < GROUP - 1, 1.0, 0.0)
        wide[pl.ds(0, EDGE), :] = halo[0].astype(jnp.float32) * has_left
        wide[pl.ds(EDGE + TOK, EDGE), :] = halo[1].astype(jnp.float32) * has_right
        offset = e * TOK + lax.broadcasted_iota(jnp.int32, (TOK, 1), 0)
        live = jnp.where(offset < length, 1.0, 0.0)

        def columns_step(i, _):
            columns = pl.ds(pl.multiple_of(i * 128, 128), 128)
            total = jnp.zeros((TOK, 128), jnp.float32)
            for tap in range(K):
                total = total + taps_ref[pl.ds(tap, 1), columns] * wide[pl.ds(EDGE - MARGIN + tap, TOK), columns]
            total = total + bias_ref[:, columns]
            mixed[:, columns] = (
                frames_ref[:, columns].astype(jnp.float32) + live * silu(total)
            ).astype(jnp.bfloat16)
            return _

        lax.fori_loop(0, D // 128, columns_step, 0)

        def second_norm(i, _):
            rows = pl.ds(pl.multiple_of(i * TILE, TILE), TILE)
            value = layer_norm(mixed[rows, :].astype(jnp.float32), ffn_gain_ref[...])
            agx[z, rows, :] = value.astype(jnp.bfloat16)
            return _

        lax.fori_loop(0, TOK // TILE, second_norm, 0)
        for way in range(2):
            ring(1, way).start()

        logits = lax.dot_general(
            router_ref[...], agx[z], (((0,), (1,)), ((), ())), preferred_element_type=jnp.float32
        )
        experts_iota = lax.broadcasted_iota(jnp.int32, (GROUP, TOK), 0)
        picked = [experts_iota == ids_ref[pl.ds(k, 1), :] for k in range(2)]
        named = jnp.where(picked[0] | picked[1], 1.0, 0.0).astype(jnp.bfloat16)
        before = lax.broadcasted_iota(jnp.int32, (TOK, TOK), 0) < lax.broadcasted_iota(jnp.int32, (TOK, TOK), 1)
        earlier = jnp.dot(
            named, jnp.where(before, 1.0, 0.0).astype(jnp.bfloat16), preferred_element_type=jnp.float32
        )
        limit, place = table_ref[:, 0:1], table_ref[:, 1:2]

        def of(k, values):
            return jnp.sum(jnp.where(picked[k], values, 0.0), axis=0, keepdims=True)

        scores = [1.0 / (1.0 + jnp.exp(-of(k, logits))) for k in range(2)]
        both = scores[0] + scores[1]
        for k in range(2):
            rank = of(k, earlier)
            meta_ref[pl.ds(k, 1), :] = jnp.where(rank < of(k, limit), of(k, place) + rank, -1.0)
            gate = (scores[k] / both).astype(jnp.bfloat16)
            meta_ref[pl.ds(2 + k, 1), :] = gate.astype(jnp.float32)
        meta_ref[pl.ds(4, 4), :] = jnp.zeros((4, TOK), jnp.float32)
        agm[z] = meta_ref[...]
        lax.fori_loop(1, ZN, send_meta, 0)

    def pair_blocks(p):
        first = (z - (p + 1) % HALF + ZN) % ZN
        second = (z + 1 + p) % ZN
        return first, second

    def choices(p):
        first, second = pair_blocks(p)
        ma, mb = agm[first], agm[second]
        row = lax.broadcasted_iota(jnp.int32, (ROWS, 1), 0)
        column = lax.broadcasted_iota(jnp.int32, (1, 2 * TOK), 1)
        code = (zlo * (XY * SLOTS) + (row // (2 * SLOTS)) * SLOTS + row % SLOTS).astype(jnp.float32)
        same = (row // SLOTS) % 2 == column // TOK
        both = jnp.concatenate([ma, mb], axis=1)
        hit0 = (both[0:1] == code) & same
        hit1 = (both[1:2] == code) & same
        return hit0, hit1, both

    def dispatch(p):
        first, second = pair_blocks(p)
        hit0, hit1, _ = choices(p)
        select = jnp.where(hit0 | hit1, 1.0, 0.0).astype(jnp.bfloat16)
        rows = jnp.dot(select[:, :TOK], agx[first], preferred_element_type=jnp.float32)
        rows = rows + jnp.dot(select[:, TOK:], agx[second], preferred_element_type=jnp.float32)
        pbuf[p] = rows.astype(jnp.bfloat16)
        mine = xrow.at[p, pl.ds(pl.multiple_of(xy * 2 * SLOTS, 2 * SLOTS), 2 * SLOTS)]
        pltpu.make_async_copy(
            pbuf.at[p, pl.ds(pl.multiple_of(xy * 2 * SLOTS, 2 * SLOTS), 2 * SLOTS)], mine, plane_self.at[p]
        ).start()

        def send(i, _):
            spot = (xy + i) % XY
            pltpu.make_async_remote_copy(
                src_ref=pbuf.at[p, pl.ds(pl.multiple_of(spot * 2 * SLOTS, 2 * SLOTS), 2 * SLOTS)],
                dst_ref=mine,
                send_sem=plane_send.at[p],
                recv_sem=plane_recv.at[p],
                device_id=plane(spot),
                device_id_type=MESH,
            ).start()
            return _

        lax.fori_loop(1, XY, send, 0)

    BULK = pl.ds(0, ROWS - 2 * SLOTS)
    OWN = pl.ds(pl.multiple_of(xy * 2 * SLOTS, 2 * SLOTS), 2 * SLOTS)

    def begin(k):
        refresh_chunk(k)
        scatter_chunk(k)

    begin(0)
    begin(1)
    frame_module()
    begin(2)
    cross_chunk(0)
    for p in range(HALF):
        for way in range(2):
            ring_arrival(p + 1, way)
        if p + 2 <= HALF:
            for way in range(2):
                ring(p + 2, way).start()
        if p == 0:
            line_meta = agm.at[pl.ds(0, ZN - 1)]
            wait_bytes(line_meta, meta_recv)
        dispatch(p)
        if p < 3:
            begin(p + 3)
            cross_chunk(p + 1)
        if p == 2:
            regroup_chunk(0)
    cross_chunk(4)
    regroup_chunk(1)

    def expert_part(rows):
        gate_pre = jnp.dot(rows, fresh[0], preferred_element_type=jnp.float32) * D ** (-0.5)
        up_pre = jnp.dot(rows, fresh[1], preferred_element_type=jnp.float32) * D ** (-0.5)
        hidden = (silu(gate_pre) * up_pre).astype(jnp.bfloat16)
        return lax.dot_general(
            hidden, fresh[2], (((1,), (1,)), ((), ())), preferred_element_type=jnp.float32
        ) * FF ** (-0.5)

    def rows_copy(p):
        return pltpu.make_async_remote_copy(
            src_ref=xrow.at[p, pl.ds(0, ROWS)],
            dst_ref=xrow.at[p, pl.ds(ROWS, ROWS)],
            send_sem=x_send.at[p],
            recv_sem=x_recv.at[p],
            device_id=partner_core,
            device_id_type=MESH,
        )

    def sums_copy(p):
        return pltpu.make_async_remote_copy(
            src_ref=yoth.at[p],
            dst_ref=yin.at[p],
            send_sem=y_send.at[p],
            recv_sem=y_recv.at[p],
            device_id=partner_core,
            device_id_type=MESH,
        )

    def pass_rows(p):
        wait_bytes(xrow.at[p, BULK], plane_recv.at[p])
        pltpu.make_async_copy(pbuf.at[p, OWN], xrow.at[p, OWN], plane_self.at[p]).wait()
        rows_copy(p).start()

    def settle(p):
        sums_copy(p).wait_recv()
        yret[p] = (yown[p % 2] + yin[p].astype(jnp.float32)).astype(jnp.bfloat16)
        pltpu.make_async_copy(yret.at[p, OWN], rret.at[p, OWN], ret_self.at[p]).start()

        def send(i, _):
            spot = (xy + i) % XY
            pltpu.make_async_remote_copy(
                src_ref=yret.at[p, pl.ds(pl.multiple_of(spot * 2 * SLOTS, 2 * SLOTS), 2 * SLOTS)],
                dst_ref=rret.at[p, OWN],
                send_sem=ret_send.at[p],
                recv_sem=ret_recv.at[p],
                device_id=plane(spot),
                device_id_type=MESH,
            ).start()
            return _

        lax.fori_loop(1, XY, send, 0)

    pass_rows(0)
    for p in range(HALF):
        if p + 1 < HALF:
            pass_rows(p + 1)
        rows_copy(p).wait_recv()
        result = expert_part(xrow[p])
        yown[p % 2] = result[:ROWS]
        yoth[p] = result[ROWS:].astype(jnp.bfloat16)
        sums_copy(p).start()
        if p > 0:
            settle(p - 1)
        if p == 1:
            cross_chunk(5)
    settle(HALF - 1)
    regroup_chunk(2)

    def combine(p, _):
        bulk = rret.at[p, BULK]
        pltpu.make_async_copy(bulk, bulk, ret_recv.at[p]).wait()
        pltpu.make_async_copy(yret.at[p, OWN], rret.at[p, OWN], ret_self.at[p]).wait()
        first, second = pair_blocks(p)
        hit0, hit1, both = choices(p)
        weights = jnp.where(hit0, both[2:3], 0.0) + jnp.where(hit1, both[3:4], 0.0)
        weights = weights.T.astype(jnp.bfloat16)
        total = jnp.dot(weights, rret[p], preferred_element_type=jnp.float32)
        part[first] = total[:TOK]
        part[second] = total[TOK:]
        return _

    lax.fori_loop(0, HALF, combine, 0)

    def rs_view(ref, step, way):
        if step == 1:
            return ref.at[way, step - 1, pl.ds(way * (TOK // 2), TOK // 2)]
        return ref.at[way, step - 1]

    def rs(step, way):
        target = line((z + 1) % ZN) if way == 0 else line((z - 1 + ZN) % ZN)
        return pltpu.make_async_remote_copy(
            src_ref=rs_view(rs_out, step, way),
            dst_ref=rs_view(rs_in, step, way),
            send_sem=rs_send.at[way, step - 1],
            recv_sem=rs_recv.at[way, step - 1],
            device_id=target,
            device_id_type=MESH,
        )

    for step in range(1, HALF + 1):
        for way in range(2):
            distance = HALF + 1 - step
            owner = (z + distance) % ZN if way == 0 else (z - distance + ZN) % ZN
            half = pl.ds(way * (TOK // 2), TOK // 2)
            other_half = pl.ds((1 - way) * (TOK // 2), TOK // 2)
            if step > 1:
                rs(step - 1, way).wait_recv()
            if step == 1:
                rs_out[way, 0, half, :] = part[owner, half, :].astype(jnp.bfloat16)
            elif step == 2:
                rs_out[way, 1, half, :] = (
                    part[owner, half, :] + rs_in[way, 0, half, :].astype(jnp.float32)
                ).astype(jnp.bfloat16)
                rs_out[way, 1, other_half, :] = part[owner, other_half, :].astype(jnp.bfloat16)
            else:
                rs_out[way, step - 1] = (
                    part[owner] + rs_in[way, step - 2].astype(jnp.float32)
                ).astype(jnp.bfloat16)
            rs(step, way).start()
        if step == 1:
            regroup_chunk(3)
        if step == 3:
            regroup_chunk(4)
        if step == 4:
            regroup_chunk(5)
    for way in range(2):
        rs(HALF, way).wait_recv()
    moe = (
        part[z]
        + rs_in[0, HALF - 1].astype(jnp.float32)
        + rs_in[1, HALF - 1].astype(jnp.float32)
    )
    out_ref[...] = (mixed[...].astype(jnp.float32) + 0.5 * moe).astype(jnp.bfloat16)

    for way in range(2):
        for step in range(1, HALF + 1):
            ring(step, way).wait_send()
            rs(step, way).wait_send()
    for way in range(2):
        edge(way).wait_send()
    for k in range(CHUNKS):

        @pl.when(inner == 1)
        def _inner():
            wait_bytes(fresh_rows(k, pl.ds(0, (XY - 1) * WIDE + XY * NARROW)), send1.at[k])
            cross_copy(k, False).wait_send()
            wait_bytes(arr.at[k, MOST], send2.at[k])
            wait_bytes(out_rows(k, TALL), recv2.at[k])
            pltpu.make_async_copy(arr.at[k, local], out_rows(k, wide_rows(xy)), self2_sem.at[k]).wait()

        @pl.when(inner == 0)
        def _outer():
            wait_bytes(fresh_rows(k, pl.ds(0, XY * WIDE + (XY - 1) * NARROW)), send1.at[k])
            cross_copy(k, True).wait_send()
            wait_bytes(arr.at[k, MOST, PART], send2.at[k])
            wait_bytes(out_rows(k, TALLER), recv2.at[k])
            pltpu.make_async_copy(arr.at[k, local, PART], out_rows(k, narrow_rows(xy)), self2_sem.at[k]).wait()

    sent_meta = agm.at[pl.ds(0, ZN - 1)]
    pltpu.make_async_copy(sent_meta, sent_meta, meta_send).wait()
    for p in range(HALF):
        bulk = pbuf.at[p, BULK]
        pltpu.make_async_copy(bulk, bulk, plane_send.at[p]).wait()
        bulk = yret.at[p, BULK]
        pltpu.make_async_copy(bulk, bulk, ret_send.at[p]).wait()
        rows_copy(p).wait_send()
        sums_copy(p).wait_send()


def communicate(cap, ident, send_list, source, length, small, weights):
    bf16, f32 = jnp.bfloat16, jnp.float32
    dma = pltpu.SemaphoreType.DMA
    vmem = pl.BlockSpec(memory_space=pltpu.VMEM)
    anyspace = pl.BlockSpec(memory_space=pl.ANY)
    moved = jax.ShapeDtypeStruct((D, FLOC), bf16)
    return pl.pallas_call(
        functools.partial(kernel, cap),
        out_shape=(jax.ShapeDtypeStruct((TOK, D), bf16), moved, moved, moved),
        in_specs=[pl.BlockSpec(memory_space=pltpu.SMEM)] * 3 + [vmem] * 8 + [anyspace] * 9,
        out_specs=(vmem, anyspace, anyspace, anyspace),
        scratch_shapes=[
            pltpu.VMEM((3, 3, D, CCOL), bf16),
            pltpu.VMEM((3, D, FLOC), bf16),
            pltpu.VMEM((TOK + 2 * EDGE, D), f32),
            pltpu.VMEM((TOK, D), bf16),
            pltpu.VMEM((2, EDGE, D), bf16),
            pltpu.VMEM((TOK, D), bf16),
            pltpu.VMEM((8, TOK), f32),
        ]
        + [pltpu.VMEM((SIDE, WIDE, CCOL), bf16)] * CHUNKS
        + [pltpu.VMEM((cap, WIDE, CCOL), bf16)] * (2 * CHUNKS)
        + [
            pltpu.VMEM((CHUNKS, SIDE, WIDE, CCOL), bf16),
            pltpu.VMEM((ZN, TOK, D), bf16),
            pltpu.VMEM((ZN, 8, TOK), f32),
            pltpu.VMEM((HALF, ROWS, D), bf16),
            pltpu.VMEM((HALF, 2 * ROWS, D), bf16),
            pltpu.VMEM((2, ROWS, D), f32),
            pltpu.VMEM((HALF, ROWS, D), bf16),
            pltpu.VMEM((HALF, ROWS, D), bf16),
            pltpu.VMEM((HALF, ROWS, D), bf16),
            pltpu.VMEM((HALF, ROWS, D), bf16),
            pltpu.VMEM((ZN, TOK, D), f32),
            pltpu.VMEM((2, HALF, TOK, D), bf16),
            pltpu.VMEM((2, HALF, TOK, D), bf16),
            dma((2,)),
            dma((2,)),
            dma((3, 3)),
            dma((CHUNKS,)),
            dma((CHUNKS,)),
            dma((CHUNKS,)),
            dma((CHUNKS,)),
            dma((CHUNKS,)),
            dma((CHUNKS,)),
            dma((CHUNKS,)),
            dma((CHUNKS,)),
            dma((2, HALF)),
            dma((2, HALF)),
            dma,
            dma,
            dma((HALF,)),
            dma((HALF,)),
            dma((HALF,)),
            dma((HALF,)),
            dma((HALF,)),
            dma((HALF,)),
            dma((HALF,)),
            dma((HALF,)),
            dma((HALF,)),
            dma((HALF,)),
            dma((2, HALF)),
            dma((2, HALF)),
        ],
        compiler_params=pltpu.CompilerParams(
            collective_id=ident, has_side_effects=True, vmem_limit_bytes=64 * 1024 * 1024 - 65536
        ),
    )(send_list, source, length, *small, *weights)


def shards(
    frames,
    lengths,
    expert_ids,
    capacity,
    resident,
    partner,
    conv_gain,
    conv_kernel,
    conv_bias,
    ffn_gain,
    router,
    gate_weight,
    up_weight,
    down_weight,
    gate_mean_grad,
    gate_mean_square,
    up_mean_grad,
    up_mean_square,
    down_mean_grad,
    down_mean_square,
):
    position = lax.axis_index("expert")
    expert_iota = jnp.arange(GROUP, dtype=jnp.int32)
    old_slot = jnp.sum(
        jnp.where(resident[None, :] == expert_iota[:, None], expert_iota[None, :], 0), axis=1
    )
    place = (old_slot % ZL) * (XY * SLOTS) + (old_slot // ZL) * SLOTS
    table = jnp.stack([capacity, place], axis=1).astype(jnp.float32)
    half_of = (expert_iota % ZL) // 2
    local_of = (expert_iota // ZL) * 2 + expert_iota % 2
    same_half = half_of[:, None] == half_of[None, :]
    paired = partner[:, None] == expert_iota[None, :]
    partner_half = jnp.sum(jnp.where(paired, half_of[None, :], 0), axis=1)
    crossing = half_of != partner_half
    ahead = same_half & (local_of[None, :] < local_of[:, None]) & crossing[None, :]
    order = jnp.sum(ahead.astype(jnp.int32), axis=1)
    my_half = (position % ZL) // 2
    mine = half_of == my_half
    send_list = jnp.sum(
        jnp.where(
            (mine & crossing)[None, :] & (order[None, :] == jnp.arange(SIDE, dtype=jnp.int32)[:, None]),
            local_of[None, :],
            0,
        ),
        axis=1,
    )
    source_of = jnp.where(crossing[:, None], SIDE + order[None, :], local_of[None, :])
    source_of = jnp.sum(jnp.where(paired, source_of, 0), axis=1)
    source = jnp.sum(
        jnp.where(
            mine[None, :] & (local_of[None, :] == jnp.arange(SIDE, dtype=jnp.int32)[:, None]),
            source_of[None, :],
            0,
        ),
        axis=1,
    )
    crossings = jnp.sum(crossing.astype(jnp.int32)) // 2
    operands = (
        send_list,
        source,
        lengths,
        (
            frames,
            expert_ids.T,
            table,
            conv_gain[None],
            conv_kernel,
            conv_bias[None],
            ffn_gain[None],
            router,
        ),
        (
            gate_weight[0], gate_mean_grad[0], gate_mean_square[0],
            up_weight[0], up_mean_grad[0], up_mean_square[0],
            down_weight[0], down_mean_grad[0], down_mean_square[0],
        ),
    )
    level = sum((crossings > cap).astype(jnp.int32) for cap in CAPS[:-1])
    block_out, fresh_gate, fresh_up, fresh_down = lax.switch(
        level,
        [
            lambda operands, cap=cap, ident=ident: communicate(cap, ident, *operands)
            for ident, cap in enumerate(CAPS)
        ],
        operands,
    )
    return (block_out, fresh_gate[None], fresh_up[None], fresh_down[None])


def solution(mesh):
    placed = (
        P(("dp", "expert"), None),
        P("dp"),
        P(("dp", "expert"), None),
        P(),
        P(),
        P(),
        P(),
        P(),
        P(),
        P(),
        P(),
        P("expert", None, "dp"),
        P("expert", None, "dp"),
        P("expert", None, "dp"),
        P("expert", None, "dp"),
        P("expert", None, "dp"),
        P("expert", None, "dp"),
        P("expert", None, "dp"),
        P("expert", None, "dp"),
        P("expert", None, "dp"),
    )
    return jax.shard_map(
        shards,
        mesh=mesh,
        in_specs=placed,
        out_specs=(
            P(("dp", "expert"), None),
            P("expert", None, "dp"),
            P("expert", None, "dp"),
            P("expert", None, "dp"),
        ),
        check_vma=False,
    )
```

time: 234 us -> 203 us (0.87); the launches traced: 230 us -> 203 us
  Pallas kernels: 198 us -> 186 us
  starting transfers between devices: 11 us -> 0 us
  local copies, waits for them, and re-layouts: 11.9 us -> 8.17 us
  other arithmetic: 7.53 us -> 4.76 us
    pallas_call x1, Pallas kernels: 198 us -> 186 us  [communicate(): pl.pallas_call(functools.partial(kernel, cap), out_shape=(jax.ShapeDtypeS...]
    ppermute x2 -> x0, starting transfers between devices: 11 us -> none  [the longest x1 7.05 us: extended(): lax.ppermute(head, axis, [((i + 1) % count, i) for i in range(ends)])]
    unnamed x31 -> x10, local copies, waits for them, and re-layouts: 11 us -> 6.6 us
    reduce_sum x7 -> x5, other arithmetic: 5.46 us -> 2.48 us  [the longest x1 0.83 us: shards(): partner_half = jnp.sum(jnp.where(paired, half_of[None, :], 0), axis=1)]
  transfers between devices with their start and end apart: 2 -> 0, of which waited for: 0 -> 0; matrix products, arithmetic and copies ran while one was open for 1% -> 0% of each run, Pallas kernels for 0% -> 0%
where the time goes in v2:
time: 203 us
  Pallas kernels  186 us (92%)
  local copies, waits for them, and re-layouts  8.17 us (4%)
  other arithmetic  4.76 us (2%)
  between operations  3.39 us (2%)
    pallas_call x1, Pallas kernels, communicate(): pl.pallas_call(functools.partial(kernel, cap), out_shape=(jax.ShapeDtypeS...  186 us
    unnamed x10, local copies, waits for them, and re-layouts  6.6 us

profile of v2, /device:TPU:2, one launch (start us, length us, event | category | flops | bytes accessed | tf_op | source)
XLA Modules:
  0.0 202.6 jit_solution(9591326998186939701)
XLA Ops:
  0.6 0.0 copy-start
  0.7 0.8 select_reduce_fusion.9
  1.5 0.7 add_convert_fusion
  2.2 0.8 select_reduce_fusion.10
  3.0 0.6 convert_reduce_fusion.1
  6.3 0.2 convert_reduce_fusion
  6.5 0.7 iota_compare_fusion.1
  7.3 0.0 copy-done
  7.3 188.6 %conditional.1 = ((bf16[128,1024]{1,0:T(8,128)(2,1)}, bf16[1024,512]{1,0:T(8,128)(2,1)}, bf16[1024,512]{1,0:T(8,128)(2,1)}, bf16[1024,512]{1,0:T(8,128)(2,1)})) conditional(s32[]{:T(128)} %clamp.3, (pred[1,64]{1,0:T(4,128)(4,1)S(1)}, pred[1,64]{1,0:T(4,128)(4,1)S(1)}, s32[64]{0:T(128)S(1)}, s32[32,64]{1,0:T(8,128)S(1)}, ...), branch_computations={%region_4.8_spmd, %region_8.12_spmd, %region_12.16_spmd} | conditional | flops 28736 | bytes 343752 | solution.py:871
  7.4 0.2 select_reduce_fusion
  7.6 0.6 select_reduce_fusion.1
  8.2 0.7 copy.24.table_ref
  8.9 0.8 copy.25.router_ref
  9.7 185.7 %branch_0_fun.2 = (bf16[128,1024]{1,0:T(8,128)(2,1)}, bf16[1024,512]{1,0:T(8,128)(2,1)}, bf16[1024,512]{1,0:T(8,128)(2,1)}, bf16[1024,512]{1,0:T(8,128)(2,1)}) custom-call(s32[32]{0:T(128)} %get-tuple-element.751.send_list_ref, s32[32]{0:T(128)} %get-tuple-element.750.source_ref, s32[1]{0:T(128)} %get-tuple-element.556.length_ref, ...), custom_call_target="tpu_custom_call" | custom-call | tf_op jit(solution)/shard_map/cond/branch_0_fun/pallas_call | solution.py:728
  195.9 1.7 copy.46
  197.6 0.0 copy-start.1
  197.6 2.4 %copy.47 = bf16[1,1024,512]{2,1,0:T(8,128)(2,1)} copy(bf16[1,1024,512]{2,1,0:T(8,128)(2,1)} %bitcast.104) | data formatting | bytes 2097152
  200.0 0.0 copy-done.1
  200.0 0.0 copy-start.2
  200.0 1.0 copy.48
  200.9 0.6 copy-done.2
  201.6 1.0 copy.49
  (14 shorter events, 0.1 us)
Async XLA Ops:
  0.6 6.7 %copy-start = (bf16[1024,64]{0,1:T(8,128)(2,1)S(1)}, bf16[1024,64]{0,1:T(8,128)(2,1)}, u32[]{:S(2)}) copy-start(bf16[1024,64]{0,1:T(8,128)(2,1)} %param.33) | copy-start | bytes 393220
  197.6 2.4 %copy-start.1 = (bf16[1024,512]{1,0:T(8,128)(2,1)S(1)}, bf16[1024,512]{1,0:T(8,128)(2,1)}, u32[]{:S(2)}) copy-start(bf16[1024,512]{1,0:T(8,128)(2,1)} %get-tuple-element.654) | copy-start | bytes 3145732
  200.0 1.6 copy-start.2

commit v3 on v2

--- a/solution.py
+++ b/solution.py
@@ -34,7 +34,7 @@
 MARGIN = (K - 1) // 2
 EDGE = 16
 TILE = 32
-CAPS = (16, 20, SIDE)
+CAPS = (18, 22, SIDE)
 
 
 def layer_norm(values, gain_row):
@@ -58,12 +58,12 @@
 
 def kernel(
     cap,
-    send_list_ref,
-    source_ref,
+    plan_ref,
     length_ref,
     frames_ref,
     ids_ref,
-    table_ref,
+    resident_ref,
+    capacity_ref,
     conv_gain_ref,
     taps_ref,
     bias_ref,
@@ -173,6 +173,25 @@
         for i in range(3):
             load(c, i).start()
 
+    def refresh_chunk(k):
+        for i in range(3):
+            load(k, i).wait()
+        slot = k % 3
+
+        def tile(i, _):
+            rows = pl.ds(pl.multiple_of(i * 64, 64), 64)
+            fresh[k // 2, rows, pl.ds((k % 2) * CCOL, CCOL)] = refresh(
+                win[slot, 0, rows, :], win[slot, 1, rows, :], win[slot, 2, rows, :]
+            )
+            return _
+
+        lax.fori_loop(0, D // 64, tile, 0)
+        if k + 3 < CHUNKS:
+            for i in range(3):
+                load(k + 3, i).start()
+
+    refresh_chunk(0)
+
     length = length_ref[0]
 
     def first_norm(i, _):
@@ -253,23 +272,6 @@
     crosses_in = (cr0, cr1, cr2, cr3, cr4, cr5)
     outs = (fg_ref, fu_ref, fd_ref)
 
-    def refresh_chunk(k):
-        for i in range(3):
-            load(k, i).wait()
-        slot = k % 3
-
-        def tile(i, _):
-            rows = pl.ds(pl.multiple_of(i * 64, 64), 64)
-            fresh[k // 2, rows, pl.ds((k % 2) * CCOL, CCOL)] = refresh(
-                win[slot, 0, rows, :], win[slot, 1, rows, :], win[slot, 2, rows, :]
-            )
-            return _
-
-        lax.fori_loop(0, D // 64, tile, 0)
-        if k + 3 < CHUNKS:
-            for i in range(3):
-                load(k + 3, i).start()
-
     def fresh_rows(k, rows):
         return fresh.at[k // 2, rows, pl.ds((k % 2) * CCOL, CCOL)]
 
@@ -356,7 +358,7 @@
             pltpu.make_async_copy(fresh_rows(k, narrow_rows(xy)), got.at[local, PART], self_sem.at[k]).wait()
 
         def pick(i, _):
-            out[i] = got[send_list_ref[i]]
+            out[i] = got[plan_ref[0, i]]
             return _
 
         lax.fori_loop(0, cap, pick, 0)
@@ -381,7 +383,7 @@
             cross_copy(k, True).wait_recv()
 
         def pick(i, _):
-            index = source_ref[i]
+            index = plan_ref[1, i]
             near = got[jnp.minimum(index, SIDE - 1)]
             far = crossed[jnp.maximum(index - SIDE, 0)]
             arr[k, i] = jnp.where(index < SIDE, near, far)
@@ -452,7 +454,7 @@
             ring(1, way).start()
 
         logits = lax.dot_general(
-            router_ref[...], agx[z], (((0,), (1,)), ((), ())), preferred_element_type=jnp.float32
+            router_ref[...], agx[z], (((1,), (1,)), ((), ())), preferred_element_type=jnp.float32
         )
         experts_iota = lax.broadcasted_iota(jnp.int32, (GROUP, TOK), 0)
         picked = [experts_iota == ids_ref[pl.ds(k, 1), :] for k in range(2)]
@@ -461,7 +463,13 @@
         earlier = jnp.dot(
             named, jnp.where(before, 1.0, 0.0).astype(jnp.bfloat16), preferred_element_type=jnp.float32
         )
-        limit, place = table_ref[:, 0:1], table_ref[:, 1:2]
+        lane = lax.broadcasted_iota(jnp.int32, (GROUP, GROUP), 1)
+        line_of = lax.broadcasted_iota(jnp.int32, (GROUP, GROUP), 0)
+        spots = (lane % ZL) * (XY * SLOTS) + (lane // ZL) * SLOTS
+        place = jnp.where(resident_ref[...] == line_of, spots, 0).astype(jnp.float32)
+        place = jnp.sum(place, axis=1, keepdims=True)
+        limit = jnp.where(lane == line_of, capacity_ref[...], 0).astype(jnp.float32)
+        limit = jnp.sum(limit, axis=1, keepdims=True)
 
         def of(k, values):
             return jnp.sum(jnp.where(picked[k], values, 0.0), axis=0, keepdims=True)
@@ -527,11 +535,11 @@
         refresh_chunk(k)
         scatter_chunk(k)
 
-    begin(0)
+    scatter_chunk(0)
     begin(1)
     frame_module()
+    cross_chunk(0)
     begin(2)
-    cross_chunk(0)
     for p in range(HALF):
         for way in range(2):
             ring_arrival(p + 1, way)
@@ -541,14 +549,19 @@
         if p == 0:
             line_meta = agm.at[pl.ds(0, ZN - 1)]
             wait_bytes(line_meta, meta_recv)
+        cross_chunk(p + 1)
         dispatch(p)
-        if p < 3:
-            begin(p + 3)
-            cross_chunk(p + 1)
+        if p == 0:
+            begin(3)
+            regroup_chunk(0)
+        if p == 1:
+            begin(4)
+            regroup_chunk(1)
         if p == 2:
-            regroup_chunk(0)
-    cross_chunk(4)
-    regroup_chunk(1)
+            begin(5)
+            regroup_chunk(2)
+        if p == 3:
+            regroup_chunk(3)
 
     def expert_part(rows):
         gate_pre = jnp.dot(rows, fresh[0], preferred_element_type=jnp.float32) * D ** (-0.5)
@@ -603,20 +616,35 @@
         lax.fori_loop(1, XY, send, 0)
 
     pass_rows(0)
-    for p in range(HALF):
-        if p + 1 < HALF:
+
+    def experts(p, _):
+        @pl.when(p + 1 < HALF)
+        def _next_rows():
             pass_rows(p + 1)
+
         rows_copy(p).wait_recv()
         result = expert_part(xrow[p])
         yown[p % 2] = result[:ROWS]
         yoth[p] = result[ROWS:].astype(jnp.bfloat16)
         sums_copy(p).start()
-        if p > 0:
+
+        @pl.when(p > 0)
+        def _settle():
             settle(p - 1)
-        if p == 1:
+
+        @pl.when(p == 0)
+        def _cross():
             cross_chunk(5)
+
+        @pl.when(p == 2)
+        def _deliver():
+            regroup_chunk(4)
+
+        return _
+
+    lax.fori_loop(0, HALF, experts, 0)
     settle(HALF - 1)
-    regroup_chunk(2)
+    regroup_chunk(5)
 
     def combine(p, _):
         bulk = rret.at[p, BULK]
@@ -669,12 +697,6 @@
                     part[owner] + rs_in[way, step - 2].astype(jnp.float32)
                 ).astype(jnp.bfloat16)
             rs(step, way).start()
-        if step == 1:
-            regroup_chunk(3)
-        if step == 3:
-            regroup_chunk(4)
-        if step == 4:
-            regroup_chunk(5)
     for way in range(2):
         rs(HALF, way).wait_recv()
     moe = (
@@ -719,7 +741,75 @@
         sums_copy(p).wait_send()
 
 
-def communicate(cap, ident, send_list, source, length, small, weights):
+def plan_kernel(partner_ref, plan_ref):
+    side = (lax.axis_index("expert") % ZL) // 2
+    lane = lax.broadcasted_iota(jnp.int32, (GROUP, GROUP), 1)
+    line_of = lax.broadcasted_iota(jnp.int32, (GROUP, GROUP), 0)
+
+    def half_of(slot):
+        return (slot % ZL) // 2
+
+    def local_of(slot):
+        return (slot // ZL) * 2 + slot % 2
+
+    partner_row = jnp.broadcast_to(partner_ref[...], (GROUP, GROUP))
+    partner_column = jnp.sum(jnp.where(lane == line_of, partner_row, 0), axis=1, keepdims=True)
+    partner_column = jnp.broadcast_to(partner_column, (GROUP, GROUP))
+    crossing_row = half_of(lane) != half_of(partner_row)
+    crossing_column = half_of(line_of) != half_of(partner_column)
+
+    def crossings_ahead(slot):
+        ahead = (half_of(lane) == half_of(slot)) & (local_of(lane) < local_of(slot)) & crossing_row
+        return jnp.sum(jnp.where(ahead, 1, 0), axis=1, keepdims=True)
+
+    mine = half_of(line_of) == side
+    sends = mine & crossing_column & (crossings_ahead(line_of) == lane)
+    source = jnp.where(crossing_column, SIDE + crossings_ahead(partner_column), local_of(partner_column))
+    count = jnp.sum(jnp.where(crossing_row, 1, 0), axis=1, keepdims=True) // 2
+    level = jnp.broadcast_to(sum(jnp.where(count > cap, 1, 0) for cap in CAPS[:-1]), (GROUP, GROUP))
+    plan_ref[pl.ds(0, 1), :] = jnp.sum(jnp.where(sends, local_of(line_of), 0), axis=0, keepdims=True)
+    plan_ref[pl.ds(1, 1), :] = jnp.sum(
+        jnp.where(mine & (local_of(line_of) == lane), source, 0), axis=0, keepdims=True
+    )
+    plan_ref[pl.ds(2, 6), :] = level[:6]
+
+
+def plan(partner):
+    vmem = pl.BlockSpec(memory_space=pltpu.VMEM)
+    return pl.pallas_call(
+        plan_kernel,
+        out_shape=jax.ShapeDtypeStruct((8, GROUP), jnp.int32),
+        in_specs=[vmem],
+        out_specs=vmem,
+    )(partner[None])
+
+
+def output_kernel(*refs):
+    sources, targets, buffers, in_sem, out_sem = refs[:4], refs[4:8], refs[8:12], refs[12], refs[13]
+    fetch = [pltpu.make_async_copy(sources[i], buffers[i], in_sem.at[i]) for i in range(4)]
+    store = [pltpu.make_async_copy(buffers[i], targets[i], out_sem.at[i]) for i in range(4)]
+    for copy in fetch:
+        copy.start()
+    for i in range(4):
+        fetch[i].wait()
+        store[i].start()
+    for copy in store:
+        copy.wait()
+
+
+def write_outputs(arrays):
+    anyspace = pl.BlockSpec(memory_space=pl.ANY)
+    return pl.pallas_call(
+        output_kernel,
+        out_shape=tuple(jax.ShapeDtypeStruct(array.shape, array.dtype) for array in arrays),
+        in_specs=[anyspace] * 4,
+        out_specs=(anyspace,) * 4,
+        scratch_shapes=[pltpu.VMEM(array.shape, array.dtype) for array in arrays]
+        + [pltpu.SemaphoreType.DMA((4,)), pltpu.SemaphoreType.DMA((4,))],
+    )(*arrays)
+
+
+def communicate(cap, ident, lists, length, small, weights):
     bf16, f32 = jnp.bfloat16, jnp.float32
     dma = pltpu.SemaphoreType.DMA
     vmem = pl.BlockSpec(memory_space=pltpu.VMEM)
@@ -728,7 +818,7 @@
     return pl.pallas_call(
         functools.partial(kernel, cap),
         out_shape=(jax.ShapeDtypeStruct((TOK, D), bf16), moved, moved, moved),
-        in_specs=[pl.BlockSpec(memory_space=pltpu.SMEM)] * 3 + [vmem] * 8 + [anyspace] * 9,
+        in_specs=[pl.BlockSpec(memory_space=pltpu.SMEM)] * 2 + [vmem] * 9 + [anyspace] * 9,
         out_specs=(vmem, anyspace, anyspace, anyspace),
         scratch_shapes=[
             pltpu.VMEM((3, 3, D, CCOL), bf16),
@@ -786,7 +876,7 @@
         compiler_params=pltpu.CompilerParams(
             collective_id=ident, has_side_effects=True, vmem_limit_bytes=64 * 1024 * 1024 - 65536
         ),
-    )(send_list, source, length, *small, *weights)
+    )(lists, length, *small, *weights)
 
 
 def shards(
@@ -811,55 +901,20 @@
     down_mean_grad,
     down_mean_square,
 ):
-    position = lax.axis_index("expert")
-    expert_iota = jnp.arange(GROUP, dtype=jnp.int32)
-    old_slot = jnp.sum(
-        jnp.where(resident[None, :] == expert_iota[:, None], expert_iota[None, :], 0), axis=1
-    )
-    place = (old_slot % ZL) * (XY * SLOTS) + (old_slot // ZL) * SLOTS
-    table = jnp.stack([capacity, place], axis=1).astype(jnp.float32)
-    half_of = (expert_iota % ZL) // 2
-    local_of = (expert_iota // ZL) * 2 + expert_iota % 2
-    same_half = half_of[:, None] == half_of[None, :]
-    paired = partner[:, None] == expert_iota[None, :]
-    partner_half = jnp.sum(jnp.where(paired, half_of[None, :], 0), axis=1)
-    crossing = half_of != partner_half
-    ahead = same_half & (local_of[None, :] < local_of[:, None]) & crossing[None, :]
-    order = jnp.sum(ahead.astype(jnp.int32), axis=1)
-    my_half = (position % ZL) // 2
-    mine = half_of == my_half
-    send_list = jnp.sum(
-        jnp.where(
-            (mine & crossing)[None, :] & (order[None, :] == jnp.arange(SIDE, dtype=jnp.int32)[:, None]),
-            local_of[None, :],
-            0,
-        ),
-        axis=1,
-    )
-    source_of = jnp.where(crossing[:, None], SIDE + order[None, :], local_of[None, :])
-    source_of = jnp.sum(jnp.where(paired, source_of, 0), axis=1)
-    source = jnp.sum(
-        jnp.where(
-            mine[None, :] & (local_of[None, :] == jnp.arange(SIDE, dtype=jnp.int32)[:, None]),
-            source_of[None, :],
-            0,
-        ),
-        axis=1,
-    )
-    crossings = jnp.sum(crossing.astype(jnp.int32)) // 2
+    lists = plan(partner)
     operands = (
-        send_list,
-        source,
+        lists,
         lengths,
         (
             frames,
             expert_ids.T,
-            table,
+            resident[None],
+            capacity[None],
             conv_gain[None],
             conv_kernel,
             conv_bias[None],
             ffn_gain[None],
-            router,
+            router.T,
         ),
         (
             gate_weight[0], gate_mean_grad[0], gate_mean_square[0],
@@ -867,14 +922,16 @@
             down_weight[0], down_mean_grad[0], down_mean_square[0],
         ),
     )
-    level = sum((crossings > cap).astype(jnp.int32) for cap in CAPS[:-1])
     block_out, fresh_gate, fresh_up, fresh_down = lax.switch(
-        level,
+        lists[2, 0],
         [
             lambda operands, cap=cap, ident=ident: communicate(cap, ident, *operands)
             for ident, cap in enumerate(CAPS)
         ],
         operands,
+    )
+    block_out, fresh_gate, fresh_up, fresh_down = write_outputs(
+        (block_out, fresh_gate, fresh_up, fresh_down)
     )
     return (block_out, fresh_gate[None], fresh_up[None], fresh_down[None])
 

time: 203 us -> 186 us (0.916)
  local copies, waits for them, and re-layouts: 8.17 us -> 1.2 us
  other arithmetic: 4.76 us -> 0 us
  Pallas kernels: 186 us -> 183 us
    pallas_call x1, Pallas kernels: 186 us -> 178 us  [communicate(): pl.pallas_call(functools.partial(kernel, cap), out_shape=(jax.ShapeDtypeS...]
    unnamed x10 -> x0, local copies, waits for them, and re-layouts: 6.6 us -> none
    pallas_call x0 -> x2, Pallas kernels: none -> 4.6 us  [the longest x1 3.08 us: write_outputs(): pl.pallas_call(output_kernel, out_shape=tuple((jax.ShapeDtypeStruct(array...]
    reduce_sum x6 -> x0, other arithmetic: 3.27 us -> none  [the longest x1 0.83 us: shards(): partner_half = jnp.sum(jnp.where(paired, half_of[None, :], 0), axis=1)]
where the time goes in v3:
time: 186 us; the launch traced here: 185 us
  Pallas kernels  183 us (98%)
    pallas_call x1, Pallas kernels, communicate(): pl.pallas_call(functools.partial(kernel, cap), out_shape=(jax.ShapeDtypeS...  178 us

profile of v3, /device:TPU:2, one launch (start us, length us, event | category | flops | bytes accessed | tf_op | source)
XLA Modules:
  0.0 185.4 jit_solution(5111000515834794493)
XLA Ops:
  0.6 1.5 shard_map.219
  2.1 1.2 slice.3
  4.0 178.2 %conditional.1 = ((bf16[128,1024]{1,0:T(8,128)(2,1)}, bf16[1024,512]{1,0:T(8,128)(2,1)}, bf16[1024,512]{1,0:T(8,128)(2,1)}, bf16[1024,512]{1,0:T(8,128)(2,1)})) conditional(s32[]{:T(128)} %bitcast.1, (s32[8,64]{1,0:T(8,128)}, s32[1]{0:T(128)}, bf16[128,1024]{1,0:T(8,128)(2,1)}, s32[2,128]{1,0:T(2,128)}, s32[1,64]{1,0:T(1,128)}, ...), branch_computations={%region_0.0_spmd, %region_1.0_spmd, %region_2.0_spmd} | conditional | bytes 8 | solution.py:925
  4.0 177.9 %branch_0_fun.1 = (bf16[128,1024]{1,0:T(8,128)(2,1)}, bf16[1024,512]{1,0:T(8,128)(2,1)}, bf16[1024,512]{1,0:T(8,128)(2,1)}, bf16[1024,512]{1,0:T(8,128)(2,1)}) custom-call(s32[8,64]{1,0:T(8,128)} %get-tuple-element.120.plan_ref, s32[1]{0:T(128)} %get-tuple-element.121.length_ref, bf16[128,1024]{1,0:T(8,128)(2,1)} %get-tuple-element.122.frames_ref, ...), custom_call_target="tpu_custom_call" | custom-call | tf_op jit(solution)/shard_map/cond/branch_0_fun/pallas_call | solution.py:818
  182.2 3.1 %shard_map.220 = (bf16[128,1024]{1,0:T(8,128)(2,1)}, bf16[1024,512]{1,0:T(8,128)(2,1)}, bf16[1024,512]{1,0:T(8,128)(2,1)}, bf16[1024,512]{1,0:T(8,128)(2,1)}) custom-call(bf16[128,1024]{1,0:T(8,128)(2,1)} %get-tuple-element.192.refs_0_, bf16[1024,512]{1,0:T(8,128)(2,1)} %get-tuple-element.193.refs_1_, bf16[1024,512]{1,0:T(8,128)(2,1)} %get-tuple-element.194.refs_2_, ...), custom_call_target="tpu_custom_call" | custom-call | tf_op jit(solution)/shard_map/pallas_call | solution.py:802

commit v4 on v3

--- a/solution.py
+++ b/solution.py
@@ -549,7 +549,14 @@
         if p == 0:
             line_meta = agm.at[pl.ds(0, ZN - 1)]
             wait_bytes(line_meta, meta_recv)
-        cross_chunk(p + 1)
+        if p == 0:
+            cross_chunk(1)
+        if p == 1:
+            cross_chunk(2)
+        if p == 2:
+            cross_chunk(3)
+        if p == 3:
+            cross_chunk(4)
         dispatch(p)
         if p == 0:
             begin(3)
@@ -633,11 +640,11 @@
             settle(p - 1)
 
         @pl.when(p == 0)
-        def _cross():
+        def _slot0():
             cross_chunk(5)
 
         @pl.when(p == 2)
-        def _deliver():
+        def _slot2():
             regroup_chunk(4)
 
         return _
@@ -646,7 +653,7 @@
     settle(HALF - 1)
     regroup_chunk(5)
 
-    def combine(p, _):
+    def combine(p):
         bulk = rret.at[p, BULK]
         pltpu.make_async_copy(bulk, bulk, ret_recv.at[p]).wait()
         pltpu.make_async_copy(yret.at[p, OWN], rret.at[p, OWN], ret_self.at[p]).wait()
@@ -657,9 +664,6 @@
         total = jnp.dot(weights, rret[p], preferred_element_type=jnp.float32)
         part[first] = total[:TOK]
         part[second] = total[TOK:]
-        return _
-
-    lax.fori_loop(0, HALF, combine, 0)
 
     def rs_view(ref, step, way):
         if step == 1:
@@ -678,6 +682,7 @@
         )
 
     for step in range(1, HALF + 1):
+        combine(HALF - step)
         for way in range(2):
             distance = HALF + 1 - step
             owner = (z + distance) % ZN if way == 0 else (z - distance + ZN) % ZN

time: 186 us -> 186 us (level)
  no operation moved by 1% of the time
where the time goes in v4:
time: 186 us
  Pallas kernels  183 us (98%)
    pallas_call x1, Pallas kernels, communicate(): pl.pallas_call(functools.partial(kernel, cap), out_shape=(jax.ShapeDtypeS...  178 us

profile of v4, /device:TPU:2, one launch (start us, length us, event | category | flops | bytes accessed | tf_op | source)
XLA Modules:
  0.0 185.6 jit_solution(12822908062131835829)
XLA Ops:
  0.6 1.5 shard_map.219
  2.1 1.2 slice.3
  4.0 178.4 %conditional.1 = ((bf16[128,1024]{1,0:T(8,128)(2,1)}, bf16[1024,512]{1,0:T(8,128)(2,1)}, bf16[1024,512]{1,0:T(8,128)(2,1)}, bf16[1024,512]{1,0:T(8,128)(2,1)})) conditional(s32[]{:T(128)} %bitcast.1, (s32[8,64]{1,0:T(8,128)}, s32[1]{0:T(128)}, bf16[128,1024]{1,0:T(8,128)(2,1)}, s32[2,128]{1,0:T(2,128)}, s32[1,64]{1,0:T(1,128)}, ...), branch_computations={%region_0.0_spmd, %region_1.0_spmd, %region_2.0_spmd} | conditional | bytes 8 | solution.py:930
  4.0 178.1 %branch_0_fun.1 = (bf16[128,1024]{1,0:T(8,128)(2,1)}, bf16[1024,512]{1,0:T(8,128)(2,1)}, bf16[1024,512]{1,0:T(8,128)(2,1)}, bf16[1024,512]{1,0:T(8,128)(2,1)}) custom-call(s32[8,64]{1,0:T(8,128)} %get-tuple-element.120.plan_ref, s32[1]{0:T(128)} %get-tuple-element.121.length_ref, bf16[128,1024]{1,0:T(8,128)(2,1)} %get-tuple-element.122.frames_ref, ...), custom_call_target="tpu_custom_call" | custom-call | tf_op jit(solution)/shard_map/cond/branch_0_fun/pallas_call | solution.py:823
  182.4 3.1 %shard_map.220 = (bf16[128,1024]{1,0:T(8,128)(2,1)}, bf16[1024,512]{1,0:T(8,128)(2,1)}, bf16[1024,512]{1,0:T(8,128)(2,1)}, bf16[1024,512]{1,0:T(8,128)(2,1)}) custom-call(bf16[128,1024]{1,0:T(8,128)(2,1)} %get-tuple-element.192.refs_0_, bf16[1024,512]{1,0:T(8,128)(2,1)} %get-tuple-element.193.refs_1_, bf16[1024,512]{1,0:T(8,128)(2,1)} %get-tuple-element.194.refs_2_, ...), custom_call_target="tpu_custom_call" | custom-call | tf_op jit(solution)/shard_map/pallas_call | solution.py:807
